TPU v7x, 32 devices: a whole 2x2x4 slice. The times are simulated.
32 devices in a mesh: gx: 16 (over z, x, core), gy: 2 (over y).
Axes of the slice: x: 2, y: 2, z: 4, core: 2. Of those that a mesh axis runs over, the one named last changes fastest.
Arguments:
- fine_old: float32 [2, 3, 40, 32, 512], P(None, None, None, 'gx', 'gy'), may hold values from -6 to 6
- fine_now: float32 [2, 3, 40, 32, 512], P(None, None, None, 'gx', 'gy'), may hold values from -6 to 6
- coarse_old: float32 [2, 3, 80, 16, 256], P(None, None, None, 'gx', 'gy'), may hold values from -6 to 6
- coarse_now: float32 [2, 3, 80, 16, 256], P(None, None, None, 'gx', 'gy'), may hold values from -6 to 6
- shear_fine: float32 [40, 32, 512], P(None, 'gx', 'gy'), may hold values from 0.3 to 1.2
- lame_fine: float32 [40, 32, 512], P(None, 'gx', 'gy'), may hold values from 0.5 to 2
- shear_coarse: float32 [80, 16, 256], P(None, 'gx', 'gy'), may hold values from 0.3 to 1.2
- lame_coarse: float32 [80, 16, 256], P(None, 'gx', 'gy'), may hold values from 0.5 to 2
- topography: int32 [32, 512], P('gx', 'gy'), may hold values from 0 to 512
Outputs:
- fine_field: float32 [2, 3, 40, 32, 512], P(None, None, None, 'gx', 'gy')
- coarse_field: float32 [2, 3, 80, 16, 256], P(None, None, None, 'gx', 'gy')
- fine_kernel: float32 [40, 32, 512], P(None, 'gx', 'gy')
- coarse_kernel: float32 [80, 16, 256], P(None, 'gx', 'gy')
All inputs are finite; a program needn't handle non-finite values.
Results may differ from a plain program's by a relative error of at most 0.0003.
Values sent between devices are 32-bit elements; how exact they have to be, the bound alone decides.
A program may use at most 64 MiB of HBM per device.

v0:
```python
import functools

import jax
import jax.numpy as jnp
from jax import lax
from jax.experimental import pallas as pl
from jax.experimental.pallas import tpu as pltpu
from jax.sharding import PartitionSpec as P

STEPS = 2
STEP_SQUARED = 0.04
LANES = 128
HALF = LANES // 2
TOP = 8


def stencil(ext, s, depth, own, grid_step, half_inv, inv_sq):
    total = ext.shape[-1]
    inverse_area = 1.0 / (grid_step * grid_step)
    tilt = 0.5 / grid_step

    def rows(slot, c, shift):
        return ext[slot, c, TOP + shift : TOP + shift + depth, :]

    def across(v):
        return pltpu.roll(v, total - 1, 1)[:, :own] - pltpu.roll(v, 1, 1)[:, :own]

    xx, yy, zz, mxy, mxz, myz = [], [], [], {}, {}, {}
    for c in range(3):
        wide = rows(s, c, 0)
        mid = wide[:, :own]
        east, west = rows(s + 1, c, 0), rows(s - 1, c, 0)
        down, up = rows(s, c, 1), rows(s, c, -1)
        twice = 2.0 * mid
        xx.append((east[:, :own] - twice + west[:, :own]) * inverse_area)
        yy.append(
            (pltpu.roll(wide, total - 1, 1)[:, :own] - twice + pltpu.roll(wide, 1, 1)[:, :own])
            * inverse_area
        )
        zz.append((down[:, :own] - twice + up[:, :own]) * inv_sq[s][:, :own])
        if c != 2:
            mxy[c] = across(east - west) * (0.25 * inverse_area)
        if c != 1:
            e = (rows(s + 1, c, 1) - rows(s + 1, c, -1))[:, :own] * half_inv[s + 1][:, :own]
            w = (rows(s - 1, c, 1) - rows(s - 1, c, -1))[:, :own] * half_inv[s - 1][:, :own]
            mxz[c] = (e - w) * tilt
        if c != 0:
            myz[c] = across((down - up) * half_inv[s]) * tilt
    laplace = [xx[c] + yy[c] + zz[c] for c in range(3)]
    grad_div = [
        xx[0] + mxy[1] + mxz[2],
        mxy[0] + yy[1] + myz[2],
        mxz[0] + myz[1] + zz[2],
    ]
    return laplace, grad_div


def body(
    nx, ny, fz, cz, fy, cy,
    fold, fnow, cold, cnow, shf, laf, shc, lac, topo,
    fout, cout, fker, cker,
    fn, cn, xf, xc, xg, pk, yr, mg, jown, jx, ext, extc, ghin, ghost,
    xs, xr, gs, gr, ys, yrs, js, jr,
):
    gx, gy = lax.axis_index("gx"), lax.axis_index("gy")
    has_x = (gx > 0, gx < nx - 1)
    has_y = (gy > 0, gy < ny - 1)
    tiles = fy // LANES
    rows_c = cn.shape[2]

    barrier = pltpu.get_barrier_semaphore()
    for side in range(2):
        step = 2 * side - 1

        @pl.when(has_x[side])
        def _():
            pl.semaphore_signal(barrier, inc=1, device_id={"gx": gx + step})

        @pl.when(has_y[side])
        def _():
            pl.semaphore_signal(barrier, inc=1, device_id={"gy": gy + step})

        @pl.when(jnp.logical_not(has_x[side]))
        def _():
            xf[:, side] = jnp.zeros(xf.shape[:1] + xf.shape[2:], jnp.float32)
            xc[:, side] = jnp.zeros(xc.shape[:1] + xc.shape[2:], jnp.float32)
            xg[:, side] = jnp.zeros(xg.shape[:1] + xg.shape[2:], jnp.float32)
            jx[side] = jnp.ones(jx.shape[1:], jnp.float32)

        @pl.when(jnp.logical_not(has_y[side]))
        def _():
            yr[:, side] = jnp.zeros(yr.shape[:1] + yr.shape[2:], jnp.float32)

    def x_copies(t, f, d):
        part = pl.ds(3 * f, 3)
        dev = {"gx": gx + 2 * d - 1}
        return (
            pltpu.make_async_remote_copy(
                cn.at[t, part], xc.at[t, 1 - d, part], xs.at[t, d, f, 0], xr.at[t, 1 - d, f, 0],
                device_id=dev,
            ),
            pltpu.make_async_remote_copy(
                fn.at[t, d, part], xf.at[t, 1 - d, part], xs.at[t, d, f, 1], xr.at[t, 1 - d, f, 1],
                device_id=dev,
            ),
        )

    def x_wait_copies(t, f, d):
        part = pl.ds(3 * f, 3)
        dev = {"gx": gx + 2 * d - 1}
        return (
            pltpu.make_async_remote_copy(
                cn.at[t, part], xc.at[t, d, part], xs.at[t, d, f, 0], xr.at[t, d, f, 0],
                device_id=dev,
            ),
            pltpu.make_async_remote_copy(
                fn.at[t, d, part], xf.at[t, d, part], xs.at[t, d, f, 1], xr.at[t, d, f, 1],
                device_id=dev,
            ),
        )

    def g_copy(t, d, land):
        return pltpu.make_async_remote_copy(
            mg.at[t], xg.at[t, land], gs.at[t, d], gr.at[t, land], device_id={"gx": gx + 2 * d - 1}
        )

    def y_copy(t, d, land):
        return pltpu.make_async_remote_copy(
            pk.at[t, d], yr.at[t, land], ys.at[t, d], yrs.at[t, land],
            device_id={"gy": gy + 2 * d - 1},
        )

    def j_copy(d, land):
        return pltpu.make_async_remote_copy(
            jown, jx.at[land], js.at[d], jr.at[land], device_id={"gx": gx + 2 * d - 1}
        )

    def each(flags, action):
        for d in range(2):
            pl.when(flags[d])(functools.partial(action, d))

    def send_x(t, f):
        def go(d):
            for copy in x_copies(t, f, d):
                copy.start()

        each(has_x, go)

    lane_f = lax.broadcasted_iota(jnp.int32, (fz, LANES), 1)
    lane_c = lax.broadcasted_iota(jnp.int32, (rows_c, LANES), 1)

    pair_row = lax.broadcasted_iota(jnp.int32, (fy, cy), 0)
    pair_col = lax.broadcasted_iota(jnp.int32, (fy, cy), 1)
    pairs = jnp.where(pair_row // 2 == pair_col, 0.25, 0.0).astype(jnp.float32)
    src = lax.broadcasted_iota(jnp.int32, (cy + LANES, fy + LANES), 0)
    dst = lax.broadcasted_iota(jnp.int32, (cy + LANES, fy + LANES), 1)
    src = jnp.where(src == cy + LANES - 1, -1, src)
    dst = jnp.where(dst == fy + LANES - 1, -1, dst)
    near = (dst + 2) // 2 - 1
    other = near + 2 * (dst + 2 - 2 * (near + 1)) - 1
    spread = jnp.where(src == near, 0.75, jnp.where(src == other, 0.25, 0.0)).astype(jnp.float32)

    def dot(a, b):
        return lax.dot_general(
            a, b, (((1,), (0,)), ((), ())),
            precision=lax.Precision.HIGHEST, preferred_element_type=jnp.float32,
        )

    def set_ridge(t, f):
        ghin[...] = jnp.zeros(ghin.shape, jnp.float32)
        for c in range(3):
            i = 3 * f + c
            ghin[c : c + 1, :fy] = fn[t, 0, i, fz - 1 : fz, :] + fn[t, 1, i, fz - 1 : fz, :]
        ridge = dot(ghin[0:8, :fy], pairs)
        for c in range(3):
            cn[t, 3 * f + c, cz : cz + 8, :] = jnp.broadcast_to(ridge[c : c + 1], (8, cy))

    jown[...] = jnp.ones(jown.shape, jnp.float32)
    jown[0:2, :] = 1.0 + topo[...].astype(jnp.float32) * (1.0 / 1024.0)
    for f in range(2):
        for i in range(3 * f, 3 * f + 3):
            cn[0, i, 0:cz, :] = cnow[i]
            for x in range(2):
                for y in range(tiles):
                    fn[0, x, i, :, y * LANES : (y + 1) * LANES] = fnow[
                        i, pl.ds(2 * y + x, fz, stride=2 * tiles), :
                    ]
        set_ridge(0, f)
    count = sum(h.astype(jnp.int32) for h in has_x + has_y)
    pl.semaphore_wait(barrier, count)
    each(has_x, lambda d: j_copy(d, 1 - d).start())
    send_x(0, 0)

    def pack(t):
        for d in range(2):
            base = HALF * (1 - d)
            at = (0, fy - 1)[d]
            fine = jnp.zeros((fz, LANES), jnp.float32)
            for i in range(6):
                for x in range(2):
                    fine = jnp.where(lane_f == base + 2 * i + x, fn[t, x, i, :, at : at + 1], fine)
            if t == 0:
                for x in range(2):
                    fine = jnp.where(
                        lane_f == base + 12 + x, jown[x : x + 1, at : at + 1], fine
                    )
            coarse = jnp.zeros((rows_c, LANES), jnp.float32)
            at = (0, cy - 1)[d]
            for i in range(6):
                coarse = jnp.where(lane_c == base + i, cn[t, i, :, at : at + 1], coarse)
            pk[t, d, 0:fz, :] = fine
            pk[t, d, fz : fz + rows_c, :] = coarse

    def exchange_columns(t):
        pack(t)
        each(has_y, lambda d: y_copy(t, d, 1 - d).start())
        each(has_y, lambda d: y_copy(t, d, d).wait_recv())
        low = lax.broadcasted_iota(jnp.int32, mg.shape[1:], 1) < HALF
        mg[t] = jnp.where(low, yr[t, 0], yr[t, 1])
        each(has_x, lambda d: g_copy(t, d, 1 - d).start())

    exchange_columns(0)
    send_x(0, 1)

    def halo_tile(v, k, lane):
        return jnp.where(
            lane == 0,
            v[:, HALF + k : HALF + k + 1],
            jnp.where(lane == LANES - 1, v[:, k : k + 1], 0.0),
        )

    each(has_x, lambda d: j_copy(d, d).wait_recv())
    lane_1 = lax.broadcasted_iota(jnp.int32, (1, LANES), 1)
    half_inv, inv_sq = {}, {}
    for q in range(4):
        if q in (0, 3):
            row = jx[0, 1:2, :] if q == 0 else jx[1, 0:1, :]
            edge = jnp.ones((1, LANES), jnp.float32)
        else:
            row = jown[q - 1 : q, :]
            head = mg[0, 0:8, :][0:1]
            edge = halo_tile(head, 12 + q - 1, lane_1)
            edge = jnp.where(edge == 0.0, 1.0, edge)
        row = jnp.concatenate([row, edge], axis=1)
        half_inv[q] = 0.5 / row
        inv_sq[q] = 1.0 / (row * row)
    half_c = {q: jnp.full((1, cy + LANES), 0.25, jnp.float32) for q in range(3)}
    sq_c = {q: jnp.full((1, cy + LANES), 0.25, jnp.float32) for q in range(3)}

    lane_g = lax.broadcasted_iota(jnp.int32, (16, fy + LANES), 1)
    row_g = lax.broadcasted_iota(jnp.int32, (16, fy + LANES), 0)
    keep = (lane_g < fy)
    keep = keep | ((lane_g == fy) & has_y[1]) | ((lane_g == fy + LANES - 1) & has_y[0])
    keep = keep & ((row_g >= 3) | has_x[0]) & ((row_g < 9) | has_x[1])

    for t in range(STEPS):
        for f in range(2):
            if t > 0 and f == 0:
                exchange_columns(t)
                send_x(t, 1)

            def coarse_in(d):
                x_wait_copies(t, f, d)[0].wait_recv()
                if f == 0:
                    g_copy(t, d, d).wait_recv()

            each(has_x, coarse_in)
            for q in range(3):
                cols = mg.at[t] if q == 1 else xg.at[t, q // 2]
                cols = cols[fz : fz + rows_c, :]
                for c in range(3):
                    i = 3 * f + c
                    plane = cn[t, i] if q == 1 else xc[t, q // 2, i]
                    whole = jnp.concatenate([plane, halo_tile(cols, i, lane_c)], axis=1)
                    extc[q, c, TOP : TOP + cz, :] = whole[0:cz]
                    extc[q, c, TOP - 1 : TOP, :] = whole[cz : cz + 1]
                    extc[q, c, TOP + cz : TOP + cz + 1, :] = jnp.zeros((1, cy + LANES), jnp.float32)
            laplace, grad_div = stencil(extc, 1, cz, cy, 2.0, half_c, sq_c)
            for c in range(3):
                i = 3 * f + c
                before = cold[i] if t == 0 else cn[t - 1, i, 0:cz, :]
                mu = shc[...]
                new = 2.0 * cn[t, i, 0:cz, :] - before + STEP_SQUARED * (
                    mu * laplace[c] + (lac[...] + mu) * grad_div[c]
                )
                if t < STEPS - 1:
                    cn[t + 1, i, 0:cz, :] = new
                else:
                    cout[i] = new

            ghin[...] = jnp.zeros(ghin.shape, jnp.float32)
            for c in range(3):
                low, mid, high = (extc[q, c, TOP : TOP + 1, :] for q in range(3))
                quads = (
                    0.75 * low + 0.25 * mid,
                    0.75 * mid + 0.25 * low,
                    0.75 * mid + 0.25 * high,
                    0.75 * high + 0.25 * mid,
                )
                for q in range(4):
                    ghin[3 * q + c : 3 * q + c + 1, : cy + LANES] = quads[q]
            ghost[...] = jnp.where(keep, dot(ghin[:, : cy + LANES], spread), 0.0)

            each(has_x, lambda d: x_wait_copies(t, f, d)[1].wait_recv())
            for q in range(4):
                cols = xg[t, q // 3, 0:fz, :] if q in (0, 3) else mg[t, 0:fz, :]
                x = (1, 0, 1, 0)[q]
                for c in range(3):
                    i = 3 * f + c
                    plane = xf[t, q // 3, i] if q in (0, 3) else fn[t, x, i]
                    whole = jnp.concatenate([plane, halo_tile(cols, 2 * i + x, lane_f)], axis=1)
                    ext[q, c, TOP : TOP + fz, :] = whole
                    ext[q, c, TOP - 1 : TOP, :] = whole[0:1]
                    ext[q, c, TOP + fz : TOP + fz + 1, :] = ghost[3 * q + c : 3 * q + c + 1, :]
            for x in range(2):
                laplace, grad_div = stencil(ext, x + 1, fz, fy, 1.0, half_inv, inv_sq)
                picks = [pl.ds(2 * y + x, fz, stride=2 * tiles) for y in range(tiles)]

                def fetch(*at):
                    return jnp.concatenate([at[0][at[1:] + (p, slice(None))] for p in picks], axis=1)

                mu = fetch(shf)
                both = fetch(laf) + mu
                for c in range(3):
                    i = 3 * f + c
                    before = fetch(fold, i) if t == 0 else fn[t - 1, x, i]
                    new = 2.0 * fn[t, x, i] - before + STEP_SQUARED * (
                        mu * laplace[c] + both * grad_div[c]
                    )
                    fn[t + 1, x, i] = new
                    if t == STEPS - 1:
                        for y in range(tiles):
                            fout[i, picks[y], :] = new[:, y * LANES : (y + 1) * LANES]
            if t < STEPS - 1:
                set_ridge(t + 1, f)
                if f == 0:
                    send_x(t + 1, 0)

        def later(i):
            return cn[t + 1, i, 0:cz, :] if t < STEPS - 1 else cout[i]

        prod = later(0) * later(3) + later(1) * later(4) + later(2) * later(5)
        cker[...] = prod if t == 0 else cker[...] + prod
        for x in range(2):
            prod = sum(fn[t + 1, x, c] * fn[t + 1, x, c + 3] for c in range(3))
            for y in range(tiles):
                piece = prod[:, y * LANES : (y + 1) * LANES]
                pick = pl.ds(2 * y + x, fz, stride=2 * tiles)
                fker[pick, :] = piece if t == 0 else fker[pick, :] + piece

    def finish_x(d):
        j_copy(d, d).wait_send()
        for t in range(STEPS):
            g_copy(t, d, d).wait_send()
            for f in range(2):
                for copy in x_wait_copies(t, f, d):
                    copy.wait_send()

    def finish_y(d):
        for t in range(STEPS):
            y_copy(t, d, d).wait_send()

    each(has_x, finish_x)
    each(has_y, finish_y)


def rows_view(a):
    lead = a.shape[:-3]
    fz, fx, fy = a.shape[-3:]
    n = len(lead)
    a = a.reshape(lead + (fz, fx, fy // LANES, LANES))
    a = a.transpose(tuple(range(n)) + (n, n + 2, n + 1, n + 3))
    return a.reshape(((6,) if lead else ()) + (fz * fx * fy // LANES, LANES))


def rows_back(a, shape):
    lead = shape[:-3]
    fz, fx, fy = shape[-3:]
    n = len(lead)
    a = a.reshape(lead + (fz, fy // LANES, fx, LANES))
    a = a.transpose(tuple(range(n)) + (n, n + 2, n + 1, n + 3))
    return a.reshape(shape)


def on_device(fold, fnow, cold, cnow, shf, laf, shc, lac, topo):
    nx, ny = lax.axis_size("gx"), lax.axis_size("gy")
    fz, fx, fy = shf.shape
    cz, cx, cy = shc.shape
    if fx != 2 or cx != 1 or cy != LANES or fy != 2 * cy:
        raise ValueError("unsupported tile")
    rows_c = cz + 8
    f32 = jnp.float32
    dma = pltpu.SemaphoreType.DMA
    nrows = fz * fx * fy // LANES
    vm = pl.BlockSpec(memory_space=pltpu.VMEM)
    fout, cout, fker, cker = pl.pallas_call(
        functools.partial(body, nx, ny, fz, cz, fy, cy),
        out_shape=(
            jax.ShapeDtypeStruct((6, nrows, LANES), f32),
            jax.ShapeDtypeStruct((6, cz, cy), f32),
            jax.ShapeDtypeStruct((nrows, LANES), f32),
            jax.ShapeDtypeStruct((cz, cy), f32),
        ),
        in_specs=[vm] * 9,
        out_specs=(vm,) * 4,
        scratch_shapes=[
            pltpu.VMEM((STEPS + 1, 2, 6, fz, fy), f32),
            pltpu.VMEM((STEPS, 6, rows_c, cy), f32),
            pltpu.VMEM((STEPS, 2, 6, fz, fy), f32),
            pltpu.VMEM((STEPS, 2, 6, rows_c, cy), f32),
            pltpu.VMEM((STEPS, 2, fz + rows_c, LANES), f32),
            pltpu.VMEM((STEPS, 2, fz + rows_c, LANES), f32),
            pltpu.VMEM((STEPS, 2, fz + rows_c, LANES), f32),
            pltpu.VMEM((STEPS, fz + rows_c, LANES), f32),
            pltpu.VMEM((8, fy), f32),
            pltpu.VMEM((2, 8, fy), f32),
            pltpu.VMEM((4, 3, fz + 16, fy + LANES), f32),
            pltpu.VMEM((3, 3, cz + 16, cy + LANES), f32),
            pltpu.VMEM((16, max(fy, cy + LANES)), f32),
            pltpu.VMEM((16, fy + LANES), f32),
            dma((STEPS, 2, 2, 2)),
            dma((STEPS, 2, 2, 2)),
            dma((STEPS, 2)),
            dma((STEPS, 2)),
            dma((STEPS, 2)),
            dma((STEPS, 2)),
            dma((2,)),
            dma((2,)),
        ],
        compiler_params=pltpu.CompilerParams(collective_id=0, has_side_effects=True),
        name="wave",
    )(
        rows_view(fold),
        rows_view(fnow),
        cold.reshape(6, cz, cy),
        cnow.reshape(6, cz, cy),
        rows_view(shf),
        rows_view(laf),
        shc.reshape(cz, cy),
        lac.reshape(cz, cy),
        topo,
    )
    return (
        rows_back(fout, fold.shape),
        cout.reshape(cold.shape),
        rows_back(fker, shf.shape),
        cker.reshape(shc.shape),
    )


def solution(mesh):
    field, coef = P(None, None, None, "gx", "gy"), P(None, "gx", "gy")
    return jax.shard_map(
        on_device,
        mesh=mesh,
        in_specs=(field,) * 4 + (coef,) * 4 + (P("gx", "gy"),),
        out_specs=(field, field, coef, coef),
        check_vma=False,
    )
```

profile of v0, /device:TPU:10, one launch (start us, length us, event | category | flops | bytes accessed | tf_op | source)
XLA Modules:
  0.0 39.9 jit_solution(9663173620358010289)
XLA Ops:
  0.6 34.8 %wave.1 = (f32[6,160,128]{2,1,0:T(8,128)}, f32[6,80,128]{2,1,0:T(8,128)}, f32[160,128]{1,0:T(8,128)}, f32[80,128]{1,0:T(8,128)}) custom-call(f32[6,160,128]{2,1,0:T(8,128)} %bitcast.41, f32[6,160,128]{2,1,0:T(8,128)} %bitcast.42, f32[6,80,128]{2,1,0:T(8,128)} %bitcast.43, f32[6,80,128]{2,1,0:T(8,128)} %bitcast.44, f32[160,128]{1,0:T(8,128)} %bitcast.47, ...), custom_call_target="tpu_custom_call" | custom-call | tf_op jit(solution)/shard_map/wave/pallas_call | solution.py:396
  35.5 0.0 copy-start
  35.5 2.0 %copy.25 = f32[2,3,40,2,256]{4,3,2,1,0:T(2,128)} copy(f32[2,3,40,2,256]{4,3,2,1,0:T(2,128)} %bitcast.40) | data formatting | bytes 983040
  37.5 0.0 copy-done
  37.5 0.0 copy-start.1
  37.5 0.7 %copy.26 = f32[2,3,80,1,128]{4,3,2,1,0:T(1,128)} copy(f32[2,3,80,1,128]{4,3,2,1,0:T(1,128)S(1)} %bitcast.45) | data formatting | bytes 491520
  38.2 0.2 copy-done.1
  38.5 0.0 copy-start.2
  38.5 0.6 %copy.27 = f32[40,2,256]{2,1,0:T(2,128)} copy(f32[40,2,256]{2,1,0:T(2,128)S(1)} %bitcast.46) | data formatting | bytes 163840
  39.1 0.1 copy-done.2
  39.2 0.6 %copy.28 = f32[80,1,128]{2,1,0:T(1,128)} copy(f32[80,1,128]{2,1,0:T(1,128)S(1)} %bitcast.49) | data formatting | bytes 81920
Async XLA Ops:
  35.5 2.0 %copy-start = (f32[6,80,128]{2,1,0:T(8,128)S(1)}, f32[6,80,128]{2,1,0:T(8,128)}, u32[]{:S(2)}) copy-start(f32[6,80,128]{2,1,0:T(8,128)} %get-tuple-element.9) | copy-start | bytes 737284
  37.5 0.9 %copy-start.1 = (f32[160,128]{1,0:T(8,128)S(1)}, f32[160,128]{1,0:T(8,128)}, u32[]{:S(2)}) copy-start(f32[160,128]{1,0:T(8,128)} %get-tuple-element.10) | copy-start | bytes 245764
  38.5 0.8 %copy-start.2 = (f32[80,128]{1,0:T(8,128)S(1)}, f32[80,128]{1,0:T(8,128)}, u32[]{:S(2)}) copy-start(f32[80,128]{1,0:T(8,128)} %get-tuple-element.11) | copy-start | bytes 122884
where the time goes:
time: 40.1 us; the launch traced here: 39.9 us
  Pallas kernels  34.8 us (87%)
  local copies, waits for them, and re-layouts  4.35 us (11%)
  between operations  0.65 us (2%)
    pallas_call x1, Pallas kernels, on_device(): pl.pallas_call(functools.partial(body, nx, ny, fz, cz, fy, cy), out_shape...  34.8 us
    unnamed x10, local copies, waits for them, and re-layouts  4.35 us

commit v1 on v0

--- a/solution.py
+++ b/solution.py
@@ -396,10 +396,10 @@
     fout, cout, fker, cker = pl.pallas_call(
         functools.partial(body, nx, ny, fz, cz, fy, cy),
         out_shape=(
-            jax.ShapeDtypeStruct((6, nrows, LANES), f32),
-            jax.ShapeDtypeStruct((6, cz, cy), f32),
-            jax.ShapeDtypeStruct((nrows, LANES), f32),
-            jax.ShapeDtypeStruct((cz, cy), f32),
+            pltpu.VMEM((6, nrows, LANES), f32),
+            pltpu.VMEM((6, cz, cy), f32),
+            pltpu.VMEM((nrows, LANES), f32),
+            pltpu.VMEM((cz, cy), f32),
         ),
         in_specs=[vm] * 9,
         out_specs=(vm,) * 4,
@@ -427,9 +427,9 @@
             dma((2,)),
             dma((2,)),
         ],
-        compiler_params=pltpu.CompilerParams(collective_id=0, has_side_effects=True),
+        compiler_params=pltpu.CompilerParams(collective_id=0, has_side_effects=True, vmem_limit_bytes=32 << 20),
         name="wave",
-    )(
+    )(*[pltpu.with_memory_space_constraint(a, pltpu.HBM) for a in (
         rows_view(fold),
         rows_view(fnow),
         cold.reshape(6, cz, cy),
@@ -439,7 +439,24 @@
         shc.reshape(cz, cy),
         lac.reshape(cz, cy),
         topo,
-    )
+    )])
+    def copy_body(*refs):
+        ins, outs, sem = refs[:4], refs[4:8], refs[8]
+        cs = [pltpu.make_async_copy(a, b, sem.at[i]) for i, (a, b) in enumerate(zip(ins, outs))]
+        for c in cs:
+            c.start()
+        for c in cs:
+            c.wait()
+
+    fout, cout, fker, cker = pl.pallas_call(
+        copy_body,
+        out_shape=tuple(jax.ShapeDtypeStruct(a.shape, f32) for a in (fout, cout, fker, cker)),
+        in_specs=[vm] * 4,
+        out_specs=(pl.BlockSpec(memory_space=pl.ANY),) * 4,
+        scratch_shapes=[dma((4,))],
+        name="put",
+        compiler_params=pltpu.CompilerParams(vmem_limit_bytes=1 << 20),
+    )(*[pltpu.with_memory_space_constraint(a, pltpu.VMEM) for a in (fout, cout, fker, cker)])
     return (
         rows_back(fout, fold.shape),
         cout.reshape(cold.shape),

time: 40.1 us -> 35.6 us (0.89)
  local copies, waits for them, and re-layouts: 4.35 us -> 0 us
    unnamed x10 -> x0, local copies, waits for them, and re-layouts: 4.35 us -> none
    pallas_call x0 -> x1, Pallas kernels: none -> 0.93 us  [on_device(): pl.pallas_call(copy_body, out_shape=tuple((jax.ShapeDtypeStruct(a.shape,...]
    pallas_call x1, Pallas kernels: 34.8 us -> 33.9 us  [on_device(): pl.pallas_call(functools.partial(body, nx, ny, fz, cz, fy, cy), out_shape...]
where the time goes in v1:
time: 35.6 us; the launch traced here: 35.5 us
  Pallas kernels  34.9 us (98%)
  between operations  0.64 us (2%)
    pallas_call x1, Pallas kernels, on_device(): pl.pallas_call(functools.partial(body, nx, ny, fz, cz, fy, cy), out_shape...  33.9 us
    pallas_call x1, Pallas kernels, on_device(): pl.pallas_call(copy_body, out_shape=tuple((jax.ShapeDtypeStruct(a.shape,...  0.93 us

profile of v1, /device:TPU:10, one launch (start us, length us, event | category | flops | bytes accessed | tf_op | source)
XLA Modules:
  0.0 35.5 jit_solution(11305429703830533207)
XLA Ops:
  0.6 33.9 %wave.1 = (f32[6,160,128]{2,1,0:T(8,128)S(1)}, f32[6,80,128]{2,1,0:T(8,128)S(1)}, f32[160,128]{1,0:T(8,128)S(1)}, f32[80,128]{1,0:T(8,128)S(1)}) custom-call(f32[6,160,128]{2,1,0:T(8,128)} %bitcast.40, f32[6,160,128]{2,1,0:T(8,128)} %bitcast.41, f32[6,80,128]{2,1,0:T(8,128)} %bitcast.42, f32[6,80,128]{2,1,0:T(8,128)} %bitcast.43, f32[160,128]{1,0:T(8,128)} %bitcast.44, ...), custom_call_target="tpu_custom_call" | custom-call | tf_op jit(solution)/shard_map/wave/pallas_call | solution.py:396
  34.6 0.9 %put.1 = (f32[6,160,128]{2,1,0:T(8,128)}, f32[6,80,128]{2,1,0:T(8,128)}, f32[160,128]{1,0:T(8,128)}, f32[80,128]{1,0:T(8,128)}) custom-call(f32[6,160,128]{2,1,0:T(8,128)S(1)} %get-tuple-element.12.refs_0_, f32[6,80,128]{2,1,0:T(8,128)S(1)} %get-tuple-element.13.refs_1_, f32[160,128]{1,0:T(8,128)S(1)} %get-tuple-element.14.refs_2_, ...), custom_call_target="tpu_custom_call" | custom-call | tf_op jit(solution)/shard_map/put/pallas_call | solution.py:451

commit v2 on v0

v2 whole, which is shorter than its diff:
```python
import functools

import jax
import jax.numpy as jnp
from jax import lax
from jax.experimental import pallas as pl
from jax.experimental.pallas import tpu as pltpu
from jax.sharding import PartitionSpec as P

STEPS = 2
STEP_SQUARED = 0.04
LANES = 128
TOP = 8


def body(
    nx, ny, fz, cz,
    fold, fnow, cold, cnow, shf, laf, shc, lac, topo,
    fout, cout, fker, cker,
    fin, fo, co, sf, lf, sc, lc, tp,
    fn, cn, xf, xc, jm, jx, pk, yr, xk,
    rj, rj2, rjh, rjl, qs, gt, tt, gs, cor,
    ins, xs, xr, js, jr, ys, yrs,
):
    f32 = jnp.float32
    gx, gy = lax.axis_index("gx"), lax.axis_index("gy")
    has_x = (gx > 0, gx < nx - 1)
    has_y = (gy > 0, gy < ny - 1)
    rows_c = cz + 8
    rows_f = fz + 8
    low_c, low_f = TOP + cz, TOP + fz

    def each(flags, action):
        for d in range(2):
            pl.when(flags[d])(functools.partial(action, d))

    def half(f):
        return pl.ds(3 * f, 3)

    loads = {
        "f0": (fnow.at[half(0)], fin.at[half(0)]),
        "c0": (cnow.at[half(0)], cn.at[0, half(0), pl.ds(TOP, cz)]),
        "topo": (topo, tp),
        "f1": (fnow.at[half(1)], fin.at[half(1)]),
        "c1": (cnow.at[half(1)], cn.at[0, half(1), pl.ds(TOP, cz)]),
        "co": (cold, co),
        "sc": (shc, sc),
        "lc": (lac, lc),
        "fo": (fold, fo),
        "sf": (shf, sf),
        "lf": (laf, lf),
    }
    loads = {
        k: pltpu.make_async_copy(a, b, ins.at[n]) for n, (k, (a, b)) in enumerate(loads.items())
    }
    for copy in loads.values():
        copy.start()

    barrier = pltpu.get_barrier_semaphore()
    each(has_x, lambda d: pl.semaphore_signal(barrier, inc=1, device_id={"gx": gx + 2 * d - 1}))
    each(has_y, lambda d: pl.semaphore_signal(barrier, inc=1, device_id={"gy": gy + 2 * d - 1}))

    def x_copy(t, f, kind, d, land):
        if kind == 0:
            rows = pl.ds(TOP - 1, cz + 1)
            src, dst = cn.at[t, half(f), rows], xc.at[t, land, half(f), rows]
        elif kind == 1:
            rows = pl.ds(TOP, fz)
            src, dst = fn.at[t, d, half(f), :, rows], xf.at[t, land, half(f), :, rows]
        else:
            src, dst = yr.at[t, f, :, pl.ds(8 * d, 8)], xk.at[t, f, land]
        return pltpu.make_async_remote_copy(
            src, dst, xs.at[t, f, kind, d], xr.at[t, f, kind, land],
            device_id={"gx": gx + 2 * d - 1},
        )

    def y_copy(t, f, d, land):
        return pltpu.make_async_remote_copy(
            pk.at[t, f, pl.ds(16 * d, 16)], yr.at[t, f, land], ys.at[t, f, d], yrs.at[t, f, land],
            device_id={"gy": gy + 2 * d - 1},
        )

    def j_copy(d, land):
        return pltpu.make_async_remote_copy(
            jm.at[d], jx.at[land], js.at[d], jr.at[land], device_id={"gx": gx + 2 * d - 1}
        )

    def x_send(t, f, *kinds):
        def go(d):
            for kind in kinds:
                x_copy(t, f, kind, d, 1 - d).start()

        each(has_x, go)

    def x_wait(t, f, kind):
        each(has_x, lambda d: x_copy(t, f, kind, d, d).wait_recv())

    def y_send(t, f):
        each(has_y, lambda d: y_copy(t, f, d, 1 - d).start())

    def y_wait(t, f):
        each(has_y, lambda d: y_copy(t, f, d, d).wait_recv())

    lane = lax.broadcasted_iota(jnp.int32, (8, LANES), 1)
    sub = lax.broadcasted_iota(jnp.int32, (8, LANES), 0)
    first, last = lane == 0, lane == LANES - 1
    left = lane < LANES // 2
    even = lane - 2 * (lane // 2) == 0
    pair_of = lane * 2 - jnp.where(left, 0, LANES)
    half_of = (lane // 2, lane // 2 + LANES // 2)
    y_edge = (first & has_y[0]) | (last & has_y[1])

    def north(v):
        return pltpu.roll(v, LANES - 1, 1)

    def south(v):
        return pltpu.roll(v, 1, 1)

    def take(v, index):
        return jnp.take_along_axis(v, index, axis=1, mode="promise_in_bounds")

    def spread(v, at, rows):
        return jnp.broadcast_to(v[:, at : at + 1], (rows, LANES))

    for t in range(STEPS):
        for i in range(6):
            row = jnp.zeros((1, LANES), f32)
            cn[t, i, low_c : low_c + 1, :] = row
            xc[t, 0, i, low_c : low_c + 1, :] = row
            xc[t, 1, i, low_c : low_c + 1, :] = row
    cor[...] = jnp.zeros(cor.shape, f32)
    gt[...] = jnp.zeros(gt.shape, f32)
    qs[...] = jnp.zeros(qs.shape, f32)
    gs[...] = jnp.zeros(gs.shape, f32)
    jm[...] = jnp.ones(jm.shape, f32)
    for d in range(2):

        @pl.when(jnp.logical_not(has_x[d]))
        def _():
            for t in range(STEPS):
                xf[t, d] = jnp.zeros(xf.shape[2:], f32)
                xc[t, d] = jnp.zeros(xc.shape[2:], f32)
                for f in range(2):
                    xk[t, f, d] = jnp.zeros(xk.shape[3:], f32)
            jx[d] = jnp.ones(jx.shape[1:], f32)

        @pl.when(jnp.logical_not(has_y[d]))
        def _():
            for t in range(STEPS):
                for f in range(2):
                    yr[t, f, d] = jnp.zeros(yr.shape[3:], f32)

    def ridge(t, f):
        for c in range(3):
            i = 3 * f + c
            for y in range(2):
                gs[y, c : c + 1] = (
                    fn[t, 0, i, y, low_f - 1 : low_f, :] + fn[t, 1, i, y, low_f - 1 : low_f, :]
                )
        a, b = gs[0], gs[1]
        a, b = take(a + north(a), pair_of), take(b + north(b), pair_of)
        mean = 0.25 * jnp.where(left, a, b)
        for c in range(3):
            cn[t, 3 * f + c, TOP - 1 : TOP, :] = mean[c : c + 1]

    def copy_top(t, x, i):
        for y in range(2):
            fn[t, x, i, y, TOP - 1 : TOP, :] = fn[t, x, i, y, TOP : TOP + 1, :]

    def pack(t, f):
        wide = lax.broadcasted_iota(jnp.int32, (rows_c, LANES), 1)
        thin = lax.broadcasted_iota(jnp.int32, (rows_f, LANES), 1)
        out = jnp.zeros((rows_c, LANES), f32)
        fine = jnp.zeros((rows_f, LANES), f32)
        for d in range(2):
            at = (0, LANES - 1)[d]
            for c in range(3):
                i, j = 3 * f + c, 16 * d + 3 + c
                v = spread(cn[t, i, TOP - 1 : TOP - 1 + rows_c, :], at, rows_c)
                out = jnp.where((wide == j) | (wide == j + 8), v, out)
                for x in range(2):
                    v = spread(fn[t, x, i, d, TOP - 1 : TOP - 1 + rows_f, :], at, rows_f)
                    fine = jnp.where(thin == 16 * d + 8 * x + c, v, fine)
            if t == 0 and f == 0:
                for x in range(2):
                    v = jnp.broadcast_to(jm[x, d : d + 1, at : at + 1], (rows_f, LANES))
                    fine = jnp.where(thin == 16 * d + 8 * x + 6, v, fine)
        of_fine = thin - 8 * (thin // 8)
        of_fine = (of_fine < 3) | (of_fine == 6)
        qs[0:rows_f, :] = jnp.where(of_fine, fine, out[0:rows_f])
        qs[rows_f:rows_c, :] = out[rows_f:]
        pk[t, f] = jnp.transpose(qs[...])[0:32]

    def begin(f):
        loads["f%d" % f].wait()
        for c in range(3):
            i = 3 * f + c
            for x in range(2):
                for y in range(2):
                    fn[0, x, i, y, TOP : TOP + fz, :] = fin[i, pl.ds(2 * y + x, fz, stride=4), :]
                copy_top(0, x, i)
        ridge(0, f)
        loads["c%d" % f].wait()

    begin(0)
    loads["topo"].wait()
    for x in range(2):
        for y in range(2):
            jm[x, y : y + 1] = 1.0 + tp[x : x + 1, y * LANES : (y + 1) * LANES].astype(f32) * (1.0 / 1024.0)
    count = sum(h.astype(jnp.int32) for h in has_x + has_y)
    pl.semaphore_wait(barrier, count)
    each(has_x, lambda d: j_copy(d, 1 - d).start())
    x_send(0, 0, 0, 1)
    pack(0, 0)
    y_send(0, 0)
    begin(1)
    pack(0, 1)
    y_send(0, 1)
    y_wait(0, 0)
    x_send(0, 0, 2)
    x_send(0, 1, 0, 1)
    y_wait(0, 1)
    x_send(0, 1, 2)

    each(has_x, lambda d: j_copy(d, d).wait_recv())
    for q in range(4):
        for y in range(2):
            row = jx[q // 3, y : y + 1] if q in (0, 3) else jm[q - 1, y : y + 1]
            inv = jnp.broadcast_to(1.0 / row, (8, LANES))
            rj[q, y] = inv
            if q in (1, 2):
                rj2[q - 1, y] = inv * inv
    for x in range(2):
        sides = []
        for s in range(2):
            row = yr[0, 0, s, 8 * x + 6 : 8 * x + 7, 0:1]
            row = jnp.broadcast_to(1.0 / jnp.where(row == 0.0, 1.0, row), (8, LANES))
            rjh[s, x] = row
            sides.append(row)
        rjl[x] = jnp.where(left, sides[0], sides[1])

    def halos(t, f):
        inside = lane <= fz
        for s in range(2):
            own = [yr[t, f, s, 8 * x : 8 * x + 8] for x in range(2)]
            west, east = xk[t, f, 0, s], xk[t, f, 1, s]
            cross = (own[1] - west, east - own[0], east - west)

            def put(k, row):
                at = 2 * k + 1 - s
                gt[at : at + 1, :] = row

            d = north(own[0]) - south(own[0])
            for c in range(3):
                put(c, own[0][3 + c : 4 + c])
            put(3, cross[2][4:5])
            put(4, cross[2][3:4] + d[5:6])
            put(5, d[4:5])
            for x in range(2):
                v = jnp.where(inside, own[x], 0.0)
                d = (north(v) - south(v)) * rjh[s, x]
                k = 6 + 6 * x
                for c in range(3):
                    put(k + c, own[x][c : c + 1])
                put(k + 3, cross[x][1:2])
                put(k + 4, cross[x][0:1] + d[2:3])
                put(k + 5, d[1:2])
        tt[...] = jnp.transpose(gt[...])

    def item(v, k):
        return pltpu.roll(v, LANES - 1 - 2 * k, 1)

    def coarse(t, f):
        for v in range(cz // 8):
            r = TOP + 8 * v
            th = tt[8 * v + 1 : 8 * v + 9, :]
            mu = (0.25 * STEP_SQUARED) * sc[8 * v : 8 * v + 8, :]
            both = (0.25 * STEP_SQUARED) * lc[8 * v : 8 * v + 8, :] + mu
            xx, yy, zz, cross, rise, tilt, twice = [], [], [], [], [], [], []
            for c in range(3):
                i = 3 * f + c
                u = cn[t, i, r : r + 8, :]
                e, w = xc[t, 1, i, r : r + 8, :], xc[t, 0, i, r : r + 8, :]
                dn, up = cn[t, i, r + 1 : r + 9, :], cn[t, i, r - 1 : r + 7, :]
                h = item(th, c)
                u2 = 2.0 * u
                twice.append(u2)
                xx.append(e + w - u2)
                yy.append(jnp.where(last, h, north(u)) + jnp.where(first, h, south(u)) - u2)
                zz.append(dn + up - u2)
                cross.append(e - w)
                rise.append(dn - up)
                if c == 1:
                    tilt.append(None)
                else:
                    ed, eu = xc[t, 1, i, r + 1 : r + 9, :], xc[t, 1, i, r - 1 : r + 7, :]
                    wd, wu = xc[t, 0, i, r + 1 : r + 9, :], xc[t, 0, i, r - 1 : r + 7, :]
                    tilt.append((ed - eu) - (wd - wu))
            ac = []
            for k, a in enumerate((cross[1], cross[0] + rise[2], rise[1])):
                h = item(th, 3 + k)
                ac.append(jnp.where(last, h, north(a)) - jnp.where(first, h, south(a)))
            grad = (
                xx[0] + 0.25 * (ac[0] + tilt[2]),
                yy[1] + 0.25 * ac[1],
                zz[2] + 0.25 * (ac[2] + tilt[0]),
            )
            prod = None
            for c in range(3):
                i = 3 * f + c
                before = co[i, 8 * v : 8 * v + 8, :] if t == 0 else cn[t - 1, i, r : r + 8, :]
                new = (twice[c] - before) + (mu * (xx[c] + yy[c] + zz[c]) + both * grad[c])
                if t < STEPS - 1:
                    cn[t + 1, i, r : r + 8, :] = new
                else:
                    cout[i, 8 * v : 8 * v + 8, :] = new
                if f == 1:
                    if t < STEPS - 1:
                        pair = cn[t + 1, c, r : r + 8, :]
                    else:
                        pair = cout[c, 8 * v : 8 * v + 8, :]
                    prod = pair * new if prod is None else prod + pair * new
            if f == 1:
                if t > 0:
                    prod = prod + cker[8 * v : 8 * v + 8, :]
                cker[8 * v : 8 * v + 8, :] = prod

    def ghost(t, f):
        for c in range(3):
            i = 3 * f + c
            gs[0, 3 + c : 4 + c] = xc[t, 0, i, TOP : TOP + 1, :]
            gs[1, 3 + c : 4 + c] = cn[t, i, TOP : TOP + 1, :]
            gs[2, 3 + c : 4 + c] = xc[t, 1, i, TOP : TOP + 1, :]
        flat = [gs[k] for k in range(3)]
        rim = []
        for tiles in (
            [xk[t, f, 0, s] for s in range(2)],
            [yr[t, f, s, 0:8] for s in range(2)],
            [xk[t, f, 1, s] for s in range(2)],
        ):
            rim.append(jnp.where(left, spread(tiles[0], 1, 8), spread(tiles[1], 1, 8)))

        def mix(v):
            lo, mid, hi = v
            return (
                0.75 * lo + 0.25 * mid,
                0.75 * mid + 0.25 * lo,
                0.75 * mid + 0.25 * hi,
                0.75 * hi + 0.25 * mid,
            )

        for q, (v, h) in enumerate(zip(mix(flat), mix(rim))):
            a = 0.75 * v + 0.25 * jnp.where(first, h, south(v))
            b = 0.75 * v + 0.25 * jnp.where(last, h, north(v))
            for y in range(2):
                g = jnp.where(even, take(a, half_of[y]), take(b, half_of[y]))
                if q in (0, 3):
                    g = jnp.where(has_x[q // 3], g, 0.0)
                for c in range(3):
                    i = 3 * f + c
                    if q in (0, 3):
                        xf[t, q // 3, i, y, low_f : low_f + 1, :] = g[3 + c : 4 + c]
                    else:
                        fn[t, q - 1, i, y, low_f : low_f + 1, :] = g[3 + c : 4 + c]
            if q in (1, 2):
                g = jnp.where(y_edge, 0.75 * h + 0.25 * v, 0.0) * rjl[q - 1]
                cor[q - 1, 0, 7:8] = g[5:6]
                cor[q - 1, 1, 7:8] = g[4:5]

    def fine(t, f):
        for side in range(2):
            for c in (0, 2):
                for y in range(2):
                    xf[t, side, 3 * f + c, y, TOP - 1 : TOP, :] = xf[
                        t, side, 3 * f + c, y, TOP : TOP + 1, :
                    ]

        def plane(q, i, y, r):
            if q in (0, 3):
                return xf[t, q // 3, i, y, r : r + 8, :]
            return fn[t, q - 1, i, y, r : r + 8, :]

        for v in range(fz // 8):
            r = TOP + 8 * v
            th = tt[8 * v + 1 : 8 * v + 9, :]
            for x in range(2):
                q = x + 1
                xx, yy, zz, up_down, twice = {}, {}, {}, {}, {}
                va = [[None, None] for _ in range(3)]
                tilt = {}
                mid = {}
                for y in range(2):
                    inv = rj[q, y]
                    cross, rise = [], []
                    for c in range(3):
                        i = 3 * f + c
                        u = plane(q, i, y, r)
                        e, w = plane(q + 1, i, y, r), plane(q - 1, i, y, r)
                        dn, up = plane(q, i, y, r + 1), plane(q, i, y, r - 1)
                        mid[c, y] = u
                        u2 = 2.0 * u
                        twice[c, y] = u2
                        xx[c, y] = e + w - u2
                        zz[c, y] = (dn + up - u2) * rj2[x, y]
                        cross.append(e - w)
                        rise.append((dn - up) * inv if c else None)
                        if c != 1:
                            ed, eu = plane(q + 1, i, y, r + 1), plane(q + 1, i, y, r - 1)
                            wd, wu = plane(q - 1, i, y, r + 1), plane(q - 1, i, y, r - 1)
                            tilt[c, y] = (ed - eu) * rj[q + 1, y] - (wd - wu) * rj[q - 1, y]
                    va[0][y] = cross[1]
                    va[1][y] = cross[0] + rise[2]
                    va[2][y] = rise[1]

                def ends(a, b, h):
                    na, nb, sa, sb = north(a), north(b), south(a), south(b)
                    return (
                        (jnp.where(last, nb, na), jnp.where(first, h, sa)),
                        (jnp.where(last, h, nb), jnp.where(first, sa, sb)),
                    )

                k = 6 + 6 * x
                for c in range(3):
                    for y, (n, s) in enumerate(ends(mid[c, 0], mid[c, 1], item(th, k + c))):
                        yy[c, y] = n + s - twice[c, y]
                ac = {}
                for c in range(3):
                    h = item(th, k + 3 + c)
                    if c and v == fz // 8 - 1:
                        h = h + cor[x, c - 1]
                    for y, (n, s) in enumerate(ends(va[c][0], va[c][1], h)):
                        ac[c, y] = n - s
                for y in range(2):
                    pick = pl.ds(32 * v + 2 * y + x, 8, stride=4)
                    mu = STEP_SQUARED * sf[pick, :]
                    both = STEP_SQUARED * lf[pick, :] + mu
                    grad = (
                        xx[0, y] + 0.25 * (ac[0, y] + tilt[2, y]),
                        yy[1, y] + 0.25 * ac[1, y],
                        zz[2, y] + 0.25 * (ac[2, y] + tilt[0, y]),
                    )
                    prod = None
                    for c in range(3):
                        i = 3 * f + c
                        before = fo[i, pick, :] if t == 0 else fn[t - 1, x, i, y, r : r + 8, :]
                        new = (twice[c, y] - before) + (
                            mu * (xx[c, y] + yy[c, y] + zz[c, y]) + both * grad[c]
                        )
                        if t < STEPS - 1:
                            fn[t + 1, x, i, y, r : r + 8, :] = new
                        else:
                            fout[i, pick, :] = new
                        if f == 1:
                            if t < STEPS - 1:
                                pair = fn[t + 1, x, c, y, r : r + 8, :]
                            else:
                                pair = fout[c, pick, :]
                            prod = pair * new if prod is None else prod + pair * new
                    if f == 1:
                        if t > 0:
                            prod = prod + fker[pick, :]
                        fker[pick, :] = prod

    def finish_level(t, f):
        for c in range(3):
            for x in range(2):
                copy_top(t, x, 3 * f + c)
        ridge(t, f)
        x_send(t, f, 0, 1)
        pack(t, f)
        y_send(t, f)

    for t in range(STEPS):
        for f in range(2):
            x_wait(t, f, 0)
            if t == 0 and f == 0:
                for k in ("co", "sc", "lc"):
                    loads[k].wait()
            x_wait(t, f, 2)
            halos(t, f)
            coarse(t, f)
            if t > 0 and f == 0:
                y_wait(t, 1)
                x_send(t, 1, 2)
            if t < STEPS - 1 and f == 1:
                y_wait(t + 1, 0)
                x_send(t + 1, 0, 2)
            ghost(t, f)
            x_wait(t, f, 1)
            if t == 0 and f == 0:
                for k in ("fo", "sf", "lf"):
                    loads[k].wait()
            fine(t, f)
            if t < STEPS - 1:
                finish_level(t + 1, f)

    def finish_x(d):
        j_copy(d, d).wait_send()
        for t in range(STEPS):
            for f in range(2):
                for kind in range(3):
                    x_copy(t, f, kind, d, d).wait_send()

    def finish_y(d):
        for t in range(STEPS):
            for f in range(2):
                y_copy(t, f, d, d).wait_send()

    each(has_x, finish_x)
    each(has_y, finish_y)


def put_body(*refs):
    ins, outs, sem = refs[:4], refs[4:8], refs[8]
    copies = [
        pltpu.make_async_copy(a, b, sem.at[i]) for i, (a, b) in enumerate(zip(ins, outs))
    ]
    for copy in copies:
        copy.start()
    for copy in copies:
        copy.wait()


def rows_view(a):
    lead = a.shape[:-3]
    fz, fx, fy = a.shape[-3:]
    n = len(lead)
    a = a.reshape(lead + (fz, fx, fy // LANES, LANES))
    a = a.transpose(tuple(range(n)) + (n, n + 2, n + 1, n + 3))
    return a.reshape(((6,) if lead else ()) + (fz * fx * fy // LANES, LANES))


def rows_back(a, shape):
    lead = shape[:-3]
    fz, fx, fy = shape[-3:]
    n = len(lead)
    a = a.reshape(lead + (fz, fy // LANES, fx, LANES))
    a = a.transpose(tuple(range(n)) + (n, n + 2, n + 1, n + 3))
    return a.reshape(shape)


def on_device(fold, fnow, cold, cnow, shf, laf, shc, lac, topo):
    nx, ny = lax.axis_size("gx"), lax.axis_size("gy")
    fz, fx, fy = shf.shape
    cz, cx, cy = shc.shape
    if fx != 2 or cx != 1 or cy != LANES or fy != 2 * cy or fz % 8 or cz % 8 or cz + 8 > LANES:
        raise ValueError("unsupported tile")
    f32 = jnp.float32
    dma = pltpu.SemaphoreType.DMA
    nrows = fz * fx * fy // LANES
    vm = pl.BlockSpec(memory_space=pltpu.VMEM)
    hbm = pl.BlockSpec(memory_space=pl.ANY)
    shapes = ((6, nrows, LANES), (6, cz, cy), (nrows, LANES), (cz, cy))
    args = (
        rows_view(fold),
        rows_view(fnow),
        cold.reshape(6, cz, cy),
        cnow.reshape(6, cz, cy),
        rows_view(shf),
        rows_view(laf),
        shc.reshape(cz, cy),
        lac.reshape(cz, cy),
        topo,
    )
    inner = pl.pallas_call(
        functools.partial(body, nx, ny, fz, cz),
        out_shape=tuple(pltpu.VMEM(s, f32) for s in shapes),
        in_specs=[hbm] * 9,
        out_specs=(vm,) * 4,
        scratch_shapes=[
            pltpu.VMEM((6, nrows, LANES), f32),
            pltpu.VMEM((6, nrows, LANES), f32),
            pltpu.VMEM((6, cz, cy), f32),
            pltpu.VMEM((nrows, LANES), f32),
            pltpu.VMEM((nrows, LANES), f32),
            pltpu.VMEM((cz, cy), f32),
            pltpu.VMEM((cz, cy), f32),
            pltpu.VMEM((fx, fy), jnp.int32),
            pltpu.VMEM((STEPS, 2, 6, 2, fz + 16, LANES), f32),
            pltpu.VMEM((STEPS, 6, cz + 16, LANES), f32),
            pltpu.VMEM((STEPS, 2, 6, 2, fz + 16, LANES), f32),
            pltpu.VMEM((STEPS, 2, 6, cz + 16, LANES), f32),
            pltpu.VMEM((2, 8, LANES), f32),
            pltpu.VMEM((2, 8, LANES), f32),
            pltpu.VMEM((STEPS, 2, 32, LANES), f32),
            pltpu.VMEM((STEPS, 2, 2, 16, LANES), f32),
            pltpu.VMEM((STEPS, 2, 2, 2, 8, LANES), f32),
            pltpu.VMEM((4, 2, 8, LANES), f32),
            pltpu.VMEM((2, 2, 8, LANES), f32),
            pltpu.VMEM((2, 2, 8, LANES), f32),
            pltpu.VMEM((2, 8, LANES), f32),
            pltpu.VMEM((LANES, LANES), f32),
            pltpu.VMEM((LANES, LANES), f32),
            pltpu.VMEM((LANES, LANES), f32),
            pltpu.VMEM((3, 8, LANES), f32),
            pltpu.VMEM((2, 2, 8, LANES), f32),
            dma((11,)),
            dma((STEPS, 2, 3, 2)),
            dma((STEPS, 2, 3, 2)),
            dma((2,)),
            dma((2,)),
            dma((STEPS, 2, 2)),
            dma((STEPS, 2, 2)),
        ],
        compiler_params=pltpu.CompilerParams(
            collective_id=0, has_side_effects=True, vmem_limit_bytes=32 << 20
        ),
        name="wave",
    )(*[pltpu.with_memory_space_constraint(a, pltpu.HBM) for a in args])
    fout, cout, fker, cker = pl.pallas_call(
        put_body,
        out_shape=tuple(jax.ShapeDtypeStruct(s, f32) for s in shapes),
        in_specs=[vm] * 4,
        out_specs=(hbm,) * 4,
        scratch_shapes=[dma((4,))],
        compiler_params=pltpu.CompilerParams(vmem_limit_bytes=1 << 20),
        name="put",
    )(*[pltpu.with_memory_space_constraint(a, pltpu.VMEM) for a in inner])
    return (
        rows_back(fout, fold.shape),
        cout.reshape(cold.shape),
        rows_back(fker, shf.shape),
        cker.reshape(shc.shape),
    )


def solution(mesh):
    field, coef = P(None, None, None, "gx", "gy"), P(None, "gx", "gy")
    return jax.shard_map(
        on_device,
        mesh=mesh,
        in_specs=(field,) * 4 + (coef,) * 4 + (P("gx", "gy"),),
        out_specs=(field, field, coef, coef),
        check_vma=False,
    )
```

time: 40.1 us -> 31.7 us (0.79)
  the two profiles are of different devices: /device:TPU:10 before, /device:TPU:1 now
where the time goes in v2:
time: 31.7 us; the launch traced here: 31.6 us
  Pallas kernels  30.9 us (97%)
  between operations  0.64 us (2%)
    pallas_call x1, Pallas kernels, on_device(): pl.pallas_call(functools.partial(body, nx, ny, fz, cz), out_shape=tuple((...  30 us
    pallas_call x1, Pallas kernels, on_device(): pl.pallas_call(put_body, out_shape=tuple((jax.ShapeDtypeStruct(s, f32) fo...  0.93 us

profile of v2, /device:TPU:1, one launch (start us, length us, event | category | flops | bytes accessed | tf_op | source)
XLA Modules:
  0.0 31.6 jit_solution(1198344446001551907)
XLA Ops:
  0.6 30.0 %wave.1 = (f32[6,160,128]{2,1,0:T(8,128)S(1)}, f32[6,80,128]{2,1,0:T(8,128)S(1)}, f32[160,128]{1,0:T(8,128)S(1)}, f32[80,128]{1,0:T(8,128)S(1)}) custom-call(f32[6,160,128]{2,1,0:T(8,128)} %bitcast.40, f32[6,160,128]{2,1,0:T(8,128)} %bitcast.41, f32[6,80,128]{2,1,0:T(8,128)} %bitcast.42, f32[6,80,128]{2,1,0:T(8,128)} %bitcast.43, f32[160,128]{1,0:T(8,128)} %bitcast.44, ...), custom_call_target="tpu_custom_call" | custom-call | tf_op jit(solution)/shard_map/wave/pallas_call | solution.py:565
  30.6 0.9 %put.1 = (f32[6,160,128]{2,1,0:T(8,128)}, f32[6,80,128]{2,1,0:T(8,128)}, f32[160,128]{1,0:T(8,128)}, f32[80,128]{1,0:T(8,128)}) custom-call(f32[6,160,128]{2,1,0:T(8,128)S(1)} %get-tuple-element.12.refs_0_, f32[6,80,128]{2,1,0:T(8,128)S(1)} %get-tuple-element.13.refs_1_, f32[160,128]{1,0:T(8,128)S(1)} %get-tuple-element.14.refs_2_, ...), custom_call_target="tpu_custom_call" | custom-call | tf_op jit(solution)/shard_map/put/pallas_call | solution.py:610

commit v3 on v2

--- a/solution.py
+++ b/solution.py
@@ -19,8 +19,8 @@
     fout, cout, fker, cker,
     fin, fo, co, sf, lf, sc, lc, tp,
     fn, cn, xf, xc, jm, jx, pk, yr, xk,
-    rj, rj2, rjh, rjl, qs, gt, tt, gs, cor,
-    ins, xs, xr, js, jr, ys, yrs,
+    rj, rj2, rjh, rjl, qs, gt, tt, gs, cor, span, via_f, via_c,
+    ins, xs, xr, jr, ys, yrs, vs, vr,
 ):
     f32 = jnp.float32
     gx, gy = lax.axis_index("gx"), lax.axis_index("gy")
@@ -50,15 +50,38 @@
         "sf": (shf, sf),
         "lf": (laf, lf),
     }
+    slots = {"f0": 0, "c0": 1, "topo": 2, "f1": 3, "c1": 4, "co": 5, "sc": 5, "lc": 5}
     loads = {
-        k: pltpu.make_async_copy(a, b, ins.at[n]) for n, (k, (a, b)) in enumerate(loads.items())
+        k: pltpu.make_async_copy(a, b, ins.at[slots.get(k, 6)]) for k, (a, b) in loads.items()
     }
     for copy in loads.values():
         copy.start()
 
+    def drain(sem, rows):
+        part = span.at[pl.ds(0, rows)]
+        pltpu.make_async_copy(part, part, sem).wait()
+
+    planes = nx // 4 if nx % 4 == 0 else 0
+    share = [min(3, (8 * (planes - 1 - z) + planes) // (2 * planes)) for z in range(planes - 1)]
+    route = [{1: 3, 2: 2, 3: 1}, {0: 2, 1: 1, 2: 3}]
+    reach = [{m: sum(n >= least for n in share) for m, least in r.items()} for r in route]
+    at4, plane = lax.rem(gx, 4), gx // 4
+    rank = jnp.where((at4 == 1) | (at4 == 3), plane, planes - 1 - plane)
+    outer = ((at4 == 0), (at4 == 3))
+    middle = (at4 == 1) | (at4 == 2)
+    detour = [{(m, d): outer[d] & (rank < r[m]) for m in r for d in range(2)} for r in reach]
+    passes = [{m: middle & (rank < r[m]) for m in r} for r in reach]
+    from_left = at4 == 2
+    even_x = lax.rem(gx, 2) == 0
+
     barrier = pltpu.get_barrier_semaphore()
     each(has_x, lambda d: pl.semaphore_signal(barrier, inc=1, device_id={"gx": gx + 2 * d - 1}))
     each(has_y, lambda d: pl.semaphore_signal(barrier, inc=1, device_id={"gy": gy + 2 * d - 1}))
+
+    @pl.when(middle & (rank < len(share)))
+    def _():
+        source = gx + jnp.where(from_left, -2, 2)
+        pl.semaphore_signal(barrier, inc=1, device_id={"gx": source})
 
     def x_copy(t, f, kind, d, land):
         if kind == 0:
@@ -70,27 +93,67 @@
         else:
             src, dst = yr.at[t, f, :, pl.ds(8 * d, 8)], xk.at[t, f, land]
         return pltpu.make_async_remote_copy(
-            src, dst, xs.at[t, f, kind, d], xr.at[t, f, kind, land],
-            device_id={"gx": gx + 2 * d - 1},
+            src, dst, xs.at[d], xr.at[t, f, kind, land], device_id={"gx": gx + 2 * d - 1}
         )
+
+    def stop(t, m):
+        if m - 2 * (m // 2) == 1:
+            return via_f.at[t, m // 2]
+        return via_c.at[t, m // 2, :, pl.ds(0, cz + 1)]
+
+    def detour_copy(t, f, kind, d):
+        m = 2 * f + kind
+        if kind == 0:
+            src = cn.at[t, half(f), pl.ds(TOP - 1, cz + 1)]
+        else:
+            src = fn.at[t, d, half(f), :, pl.ds(TOP, fz)]
+        return pltpu.make_async_remote_copy(
+            src, stop(t, m), xs.at[d], vr.at[t, m], device_id={"gx": gx + 2 - 4 * d}
+        )
+
+    def pass_copy(t, m, land):
+        f, kind = m // 2, m - 2 * (m // 2)
+        if kind == 0:
+            dst = xc.at[t, land, half(f), pl.ds(TOP - 1, cz + 1)]
+        else:
+            dst = xf.at[t, land, half(f), :, pl.ds(TOP, fz)]
+        return pltpu.make_async_remote_copy(
+            stop(t, m), dst, vs.at[t, m], xr.at[t, f, kind, land],
+            device_id={"gx": gx + 3 - 6 * land},
+        )
+
+    def pass_on(t, m):
+        @pl.when(passes[t][m])
+        def _():
+            part = stop(t, m)
+            pltpu.make_async_copy(part, part, vr.at[t, m]).wait()
+            for land in range(2):
+                pl.when((at4 == 1 + land))(pass_copy(t, m, land).start)
 
     def y_copy(t, f, d, land):
         return pltpu.make_async_remote_copy(
-            pk.at[t, f, pl.ds(16 * d, 16)], yr.at[t, f, land], ys.at[t, f, d], yrs.at[t, f, land],
+            pk.at[t, f, pl.ds(16 * d, 16)], yr.at[t, f, land], ys.at[d], yrs.at[t, f, land],
             device_id={"gy": gy + 2 * d - 1},
         )
 
     def j_copy(d, land):
         return pltpu.make_async_remote_copy(
-            jm.at[d], jx.at[land], js.at[d], jr.at[land], device_id={"gx": gx + 2 * d - 1}
+            jm.at[d], jx.at[land], xs.at[d], jr.at[land], device_id={"gx": gx + 2 * d - 1}
         )
 
     def x_send(t, f, *kinds):
         def go(d):
             for kind in kinds:
-                x_copy(t, f, kind, d, 1 - d).start()
-
-        each(has_x, go)
+                m = 2 * f + kind
+                if kind == 2 or m not in route[t]:
+                    x_copy(t, f, kind, d, 1 - d).start()
+                else:
+                    pl.when(detour[t][m, d])(detour_copy(t, f, kind, d).start)
+                    pl.when(jnp.logical_not(detour[t][m, d]))(x_copy(t, f, kind, d, 1 - d).start)
+
+        pl.when(has_x[1] & even_x)(functools.partial(go, 1))
+        pl.when(has_x[0])(functools.partial(go, 0))
+        pl.when(has_x[1] & jnp.logical_not(even_x))(functools.partial(go, 1))
 
     def x_wait(t, f, kind):
         each(has_x, lambda d: x_copy(t, f, kind, d, d).wait_recv())
@@ -207,7 +270,7 @@
     for x in range(2):
         for y in range(2):
             jm[x, y : y + 1] = 1.0 + tp[x : x + 1, y * LANES : (y + 1) * LANES].astype(f32) * (1.0 / 1024.0)
-    count = sum(h.astype(jnp.int32) for h in has_x + has_y)
+    count = sum(h.astype(jnp.int32) for h in has_x + has_y + tuple(side & (rank < len(share)) for side in outer))
     pl.semaphore_wait(barrier, count)
     each(has_x, lambda d: j_copy(d, 1 - d).start())
     x_send(0, 0, 0, 1)
@@ -472,10 +535,11 @@
 
     for t in range(STEPS):
         for f in range(2):
+            if f == 1:
+                pass_on(t, (2, 1)[t])
             x_wait(t, f, 0)
             if t == 0 and f == 0:
-                for k in ("co", "sc", "lc"):
-                    loads[k].wait()
+                drain(ins.at[5], 8 * cz)
             x_wait(t, f, 2)
             halos(t, f)
             coarse(t, f)
@@ -486,28 +550,20 @@
                 y_wait(t + 1, 0)
                 x_send(t + 1, 0, 2)
             ghost(t, f)
+            pass_on(t, ((1, 3), (0, 2))[t][f])
             x_wait(t, f, 1)
             if t == 0 and f == 0:
-                for k in ("fo", "sf", "lf"):
-                    loads[k].wait()
+                drain(ins.at[6], 32 * fz)
             fine(t, f)
             if t < STEPS - 1:
                 finish_level(t + 1, f)
 
-    def finish_x(d):
-        j_copy(d, d).wait_send()
-        for t in range(STEPS):
-            for f in range(2):
-                for kind in range(3):
-                    x_copy(t, f, kind, d, d).wait_send()
-
-    def finish_y(d):
-        for t in range(STEPS):
-            for f in range(2):
-                y_copy(t, f, d, d).wait_send()
-
-    each(has_x, finish_x)
-    each(has_y, finish_y)
+    sent = 8 + 2 * STEPS * (3 * (cz + 1) + 6 * fz + 16)
+    each(has_x, lambda d: drain(xs.at[d], sent))
+    each(has_y, lambda d: drain(ys.at[d], 32 * STEPS))
+    for t in range(STEPS):
+        for m in route[t]:
+            pl.when(passes[t][m])(pass_copy(t, m, 0).wait_send)
 
 
 def put_body(*refs):
@@ -594,13 +650,17 @@
             pltpu.VMEM((LANES, LANES), f32),
             pltpu.VMEM((3, 8, LANES), f32),
             pltpu.VMEM((2, 2, 8, LANES), f32),
-            dma((11,)),
-            dma((STEPS, 2, 3, 2)),
+            pltpu.VMEM((4 * STEPS * (3 * cz + 6 * fz + 32), LANES), f32),
+            pltpu.VMEM((STEPS, 2, 3, 2, fz, LANES), f32),
+            pltpu.VMEM((STEPS, 2, 3, cz + 8, LANES), f32),
+            dma((7,)),
+            dma((2,)),
             dma((STEPS, 2, 3, 2)),
             dma((2,)),
             dma((2,)),
             dma((STEPS, 2, 2)),
-            dma((STEPS, 2, 2)),
+            dma((STEPS, 4)),
+            dma((STEPS, 4)),
         ],
         compiler_params=pltpu.CompilerParams(
             collective_id=0, has_side_effects=True, vmem_limit_bytes=32 << 20

time: 31.7 us -> 29.8 us (0.940)
  the two profiles are of different devices: /device:TPU:1 before, /device:TPU:19 now
where the time goes in v3:
time: 29.8 us; the launch traced here: 29.5 us
  Pallas kernels  28.8 us (97%)
  between operations  0.64 us (2%)
    pallas_call x1, Pallas kernels, on_device(): pl.pallas_call(functools.partial(body, nx, ny, fz, cz), out_shape=tuple((...  27.9 us
    pallas_call x1, Pallas kernels, on_device(): pl.pallas_call(put_body, out_shape=tuple((jax.ShapeDtypeStruct(s, f32) fo...  0.93 us

profile of v3, /device:TPU:19, one launch (start us, length us, event | category | flops | bytes accessed | tf_op | source)
XLA Modules:
  0.0 29.5 jit_solution(10145634356446586209)
XLA Ops:
  0.6 27.9 %wave.1 = (f32[6,160,128]{2,1,0:T(8,128)S(1)}, f32[6,80,128]{2,1,0:T(8,128)S(1)}, f32[160,128]{1,0:T(8,128)S(1)}, f32[80,128]{1,0:T(8,128)S(1)}) custom-call(f32[6,160,128]{2,1,0:T(8,128)} %bitcast.40, f32[6,160,128]{2,1,0:T(8,128)} %bitcast.41, f32[6,80,128]{2,1,0:T(8,128)} %bitcast.42, f32[6,80,128]{2,1,0:T(8,128)} %bitcast.43, f32[160,128]{1,0:T(8,128)} %bitcast.44, ...), custom_call_target="tpu_custom_call" | custom-call | tf_op jit(solution)/shard_map/wave/pallas_call | solution.py:621
  28.6 0.9 %put.1 = (f32[6,160,128]{2,1,0:T(8,128)}, f32[6,80,128]{2,1,0:T(8,128)}, f32[160,128]{1,0:T(8,128)}, f32[80,128]{1,0:T(8,128)}) custom-call(f32[6,160,128]{2,1,0:T(8,128)S(1)} %get-tuple-element.12.refs_0_, f32[6,80,128]{2,1,0:T(8,128)S(1)} %get-tuple-element.13.refs_1_, f32[160,128]{1,0:T(8,128)S(1)} %get-tuple-element.14.refs_2_, ...), custom_call_target="tpu_custom_call" | custom-call | tf_op jit(solution)/shard_map/put/pallas_call | solution.py:670

commit v4 on v3

--- a/solution.py
+++ b/solution.py
@@ -535,12 +535,16 @@
 
     for t in range(STEPS):
         for f in range(2):
-            if f == 1:
-                pass_on(t, (2, 1)[t])
+            if (t, f) != (0, 0):
+                pass_on(t, {(0, 1): 2, (1, 0): 0, (1, 1): 2}[t, f])
             x_wait(t, f, 0)
+            if t == 0:
+                pass_on(0, (1, 3)[f])
             if t == 0 and f == 0:
                 drain(ins.at[5], 8 * cz)
             x_wait(t, f, 2)
+            if t == 1 and f == 0:
+                pass_on(1, 1)
             halos(t, f)
             coarse(t, f)
             if t > 0 and f == 0:
@@ -550,7 +554,6 @@
                 y_wait(t + 1, 0)
                 x_send(t + 1, 0, 2)
             ghost(t, f)
-            pass_on(t, ((1, 3), (0, 2))[t][f])
             x_wait(t, f, 1)
             if t == 0 and f == 0:
                 drain(ins.at[6], 32 * fz)

time: 29.8 us -> 27.8 us (0.933)
  Pallas kernels: 28.8 us -> 27 us
    pallas_call x1, Pallas kernels: 27.9 us -> 26.1 us  [on_device(): pl.pallas_call(functools.partial(body, nx, ny, fz, cz), out_shape=tuple((...]
where the time goes in v4:
time: 27.8 us; the launch traced here: 27.7 us
  Pallas kernels  27 us (97%)
  between operations  0.64 us (2%)
    pallas_call x1, Pallas kernels, on_device(): pl.pallas_call(functools.partial(body, nx, ny, fz, cz), out_shape=tuple((...  26.1 us
    pallas_call x1, Pallas kernels, on_device(): pl.pallas_call(put_body, out_shape=tuple((jax.ShapeDtypeStruct(s, f32) fo...  0.93 us

profile of v4, /device:TPU:19, one launch (start us, length us, event | category | flops | bytes accessed | tf_op | source)
XLA Modules:
  0.0 27.7 jit_solution(4415836286493803880)
XLA Ops:
  0.6 26.1 %wave.1 = (f32[6,160,128]{2,1,0:T(8,128)S(1)}, f32[6,80,128]{2,1,0:T(8,128)S(1)}, f32[160,128]{1,0:T(8,128)S(1)}, f32[80,128]{1,0:T(8,128)S(1)}) custom-call(f32[6,160,128]{2,1,0:T(8,128)} %bitcast.40, f32[6,160,128]{2,1,0:T(8,128)} %bitcast.41, f32[6,80,128]{2,1,0:T(8,128)} %bitcast.42, f32[6,80,128]{2,1,0:T(8,128)} %bitcast.43, f32[160,128]{1,0:T(8,128)} %bitcast.44, ...), custom_call_target="tpu_custom_call" | custom-call | tf_op jit(solution)/shard_map/wave/pallas_call | solution.py:624
  26.7 0.9 %put.1 = (f32[6,160,128]{2,1,0:T(8,128)}, f32[6,80,128]{2,1,0:T(8,128)}, f32[160,128]{1,0:T(8,128)}, f32[80,128]{1,0:T(8,128)}) custom-call(f32[6,160,128]{2,1,0:T(8,128)S(1)} %get-tuple-element.12.refs_0_, f32[6,80,128]{2,1,0:T(8,128)S(1)} %get-tuple-element.13.refs_1_, f32[160,128]{1,0:T(8,128)S(1)} %get-tuple-element.14.refs_2_, ...), custom_call_target="tpu_custom_call" | custom-call | tf_op jit(solution)/shard_map/put/pallas_call | solution.py:673

commit v5 on v3

--- a/solution.py
+++ b/solution.py
@@ -20,7 +20,7 @@
     fin, fo, co, sf, lf, sc, lc, tp,
     fn, cn, xf, xc, jm, jx, pk, yr, xk,
     rj, rj2, rjh, rjl, qs, gt, tt, gs, cor, span, via_f, via_c,
-    ins, xs, xr, jr, ys, yrs, vs, vr,
+    ins, xs, xr, ys, yrs, vs, vr,
 ):
     f32 = jnp.float32
     gx, gy = lax.axis_index("gx"), lax.axis_index("gy")
@@ -50,12 +50,9 @@
         "sf": (shf, sf),
         "lf": (laf, lf),
     }
-    slots = {"f0": 0, "c0": 1, "topo": 2, "f1": 3, "c1": 4, "co": 5, "sc": 5, "lc": 5}
-    loads = {
-        k: pltpu.make_async_copy(a, b, ins.at[slots.get(k, 6)]) for k, (a, b) in loads.items()
-    }
-    for copy in loads.values():
-        copy.start()
+    slots = {"f0": 0, "c0": 0, "topo": 0, "f1": 1, "c1": 1, "co": 2, "sc": 2, "lc": 2}
+    for k, (a, b) in loads.items():
+        pltpu.make_async_copy(a, b, ins.at[slots.get(k, 3)]).start()
 
     def drain(sem, rows):
         part = span.at[pl.ds(0, rows)]
@@ -63,7 +60,7 @@
 
     planes = nx // 4 if nx % 4 == 0 else 0
     share = [min(3, (8 * (planes - 1 - z) + planes) // (2 * planes)) for z in range(planes - 1)]
-    route = [{1: 3, 2: 2, 3: 1}, {0: 2, 1: 1, 2: 3}]
+    route = [{1: 3, 2: 2, 3: 1}, {0: 2, 1: 1}]
     reach = [{m: sum(n >= least for n in share) for m, least in r.items()} for r in route]
     at4, plane = lax.rem(gx, 4), gx // 4
     rank = jnp.where((at4 == 1) | (at4 == 3), plane, planes - 1 - plane)
@@ -73,6 +70,7 @@
     passes = [{m: middle & (rank < r[m]) for m in r} for r in reach]
     from_left = at4 == 2
     even_x = lax.rem(gx, 2) == 0
+    turn = jnp.where((outer[0] & has_x[0]) | (outer[1] & has_x[1]), 1, 0) if share else 0
 
     barrier = pltpu.get_barrier_semaphore()
     each(has_x, lambda d: pl.semaphore_signal(barrier, inc=1, device_id={"gx": gx + 2 * d - 1}))
@@ -91,9 +89,9 @@
             rows = pl.ds(TOP, fz)
             src, dst = fn.at[t, d, half(f), :, rows], xf.at[t, land, half(f), :, rows]
         else:
-            src, dst = yr.at[t, f, :, pl.ds(8 * d, 8)], xk.at[t, f, land]
+            src, dst = yr.at[t, f, :, pl.ds(8 * d, 4)], xk.at[t, f, land, :, pl.ds(0, 4)]
         return pltpu.make_async_remote_copy(
-            src, dst, xs.at[d], xr.at[t, f, kind, land], device_id={"gx": gx + 2 * d - 1}
+            src, dst, xs.at[d], xr.at[t, f, kind % 2, land], device_id={"gx": gx + 2 * d - 1}
         )
 
     def stop(t, m):
@@ -108,7 +106,7 @@
         else:
             src = fn.at[t, d, half(f), :, pl.ds(TOP, fz)]
         return pltpu.make_async_remote_copy(
-            src, stop(t, m), xs.at[d], vr.at[t, m], device_id={"gx": gx + 2 - 4 * d}
+            src, stop(t, m), xs.at[d], vr.at[4 * t + m], device_id={"gx": gx + 2 - 4 * d}
         )
 
     def pass_copy(t, m, land):
@@ -118,7 +116,7 @@
         else:
             dst = xf.at[t, land, half(f), :, pl.ds(TOP, fz)]
         return pltpu.make_async_remote_copy(
-            stop(t, m), dst, vs.at[t, m], xr.at[t, f, kind, land],
+            stop(t, m), dst, vs.at[0], xr.at[t, f, kind, land],
             device_id={"gx": gx + 3 - 6 * land},
         )
 
@@ -126,7 +124,7 @@
         @pl.when(passes[t][m])
         def _():
             part = stop(t, m)
-            pltpu.make_async_copy(part, part, vr.at[t, m]).wait()
+            pltpu.make_async_copy(part, part, vr.at[4 * t + m]).wait()
             for land in range(2):
                 pl.when((at4 == 1 + land))(pass_copy(t, m, land).start)
 
@@ -138,10 +136,10 @@
 
     def j_copy(d, land):
         return pltpu.make_async_remote_copy(
-            jm.at[d], jx.at[land], xs.at[d], jr.at[land], device_id={"gx": gx + 2 * d - 1}
+            jm.at[d], jx.at[land], xs.at[d], xr.at[0, 0, 0, land], device_id={"gx": gx + 2 * d - 1}
         )
 
-    def x_send(t, f, *kinds):
+    def x_send(t, f, *kinds, where=True):
         def go(d):
             for kind in kinds:
                 m = 2 * f + kind
@@ -151,12 +149,13 @@
                     pl.when(detour[t][m, d])(detour_copy(t, f, kind, d).start)
                     pl.when(jnp.logical_not(detour[t][m, d]))(x_copy(t, f, kind, d, 1 - d).start)
 
-        pl.when(has_x[1] & even_x)(functools.partial(go, 1))
-        pl.when(has_x[0])(functools.partial(go, 0))
-        pl.when(has_x[1] & jnp.logical_not(even_x))(functools.partial(go, 1))
+        pl.when(has_x[1] & even_x & where)(functools.partial(go, 1))
+        pl.when(has_x[0] & where)(functools.partial(go, 0))
+        pl.when(has_x[1] & jnp.logical_not(even_x) & where)(functools.partial(go, 1))
 
     def x_wait(t, f, kind):
-        each(has_x, lambda d: x_copy(t, f, kind, d, d).wait_recv())
+        rows = 6 * fz if kind else 3 * (cz + 1) + 8 + (8 if t == 0 and f == 0 else 0)
+        each(has_x, lambda d: drain(xr.at[t, f, kind, d], rows))
 
     def y_send(t, f):
         each(has_y, lambda d: y_copy(t, f, d, 1 - d).start())
@@ -232,30 +231,35 @@
 
     def pack(t, f):
         wide = lax.broadcasted_iota(jnp.int32, (rows_c, LANES), 1)
+        one = lax.broadcasted_iota(jnp.int32, (1, LANES), 1)
+        spare = jnp.zeros((1, LANES), f32)
         thin = lax.broadcasted_iota(jnp.int32, (rows_f, LANES), 1)
         out = jnp.zeros((rows_c, LANES), f32)
         fine = jnp.zeros((rows_f, LANES), f32)
         for d in range(2):
             at = (0, LANES - 1)[d]
             for c in range(3):
-                i, j = 3 * f + c, 16 * d + 3 + c
+                i, j = 3 * f + c, 16 * d + (2, 3, 5)[c]
                 v = spread(cn[t, i, TOP - 1 : TOP - 1 + rows_c, :], at, rows_c)
                 out = jnp.where((wide == j) | (wide == j + 8), v, out)
                 for x in range(2):
                     v = spread(fn[t, x, i, d, TOP - 1 : TOP - 1 + rows_f, :], at, rows_f)
-                    fine = jnp.where(thin == 16 * d + 8 * x + c, v, fine)
+                    fine = jnp.where(thin == 16 * d + 8 * x + (0, 1, 4)[c], v, fine)
+            j, v = 16 * d, spread(cn[t, 3 * f + 2, TOP : TOP + 1, :], at, 1)
+            spare = jnp.where((one == j) | (one == j + 8), v, spare)
             if t == 0 and f == 0:
                 for x in range(2):
                     v = jnp.broadcast_to(jm[x, d : d + 1, at : at + 1], (rows_f, LANES))
                     fine = jnp.where(thin == 16 * d + 8 * x + 6, v, fine)
         of_fine = thin - 8 * (thin // 8)
-        of_fine = (of_fine < 3) | (of_fine == 6)
+        of_fine = (of_fine < 2) | (of_fine == 4) | (of_fine == 6)
         qs[0:rows_f, :] = jnp.where(of_fine, fine, out[0:rows_f])
         qs[rows_f:rows_c, :] = out[rows_f:]
+        qs[LANES - 1 :, :] = spare
         pk[t, f] = jnp.transpose(qs[...])[0:32]
 
     def begin(f):
-        loads["f%d" % f].wait()
+        drain(ins.at[f], 12 * fz + 3 * cz + (0 if f else 4))
         for c in range(3):
             i = 3 * f + c
             for x in range(2):
@@ -263,10 +267,8 @@
                     fn[0, x, i, y, TOP : TOP + fz, :] = fin[i, pl.ds(2 * y + x, fz, stride=4), :]
                 copy_top(0, x, i)
         ridge(0, f)
-        loads["c%d" % f].wait()
 
     begin(0)
-    loads["topo"].wait()
     for x in range(2):
         for y in range(2):
             jm[x, y : y + 1] = 1.0 + tp[x : x + 1, y * LANES : (y + 1) * LANES].astype(f32) * (1.0 / 1024.0)
@@ -285,22 +287,22 @@
     y_wait(0, 1)
     x_send(0, 1, 2)
 
-    each(has_x, lambda d: j_copy(d, d).wait_recv())
-    for q in range(4):
-        for y in range(2):
-            row = jx[q // 3, y : y + 1] if q in (0, 3) else jm[q - 1, y : y + 1]
-            inv = jnp.broadcast_to(1.0 / row, (8, LANES))
-            rj[q, y] = inv
-            if q in (1, 2):
-                rj2[q - 1, y] = inv * inv
-    for x in range(2):
-        sides = []
-        for s in range(2):
-            row = yr[0, 0, s, 8 * x + 6 : 8 * x + 7, 0:1]
-            row = jnp.broadcast_to(1.0 / jnp.where(row == 0.0, 1.0, row), (8, LANES))
-            rjh[s, x] = row
-            sides.append(row)
-        rjl[x] = jnp.where(left, sides[0], sides[1])
+    def spacings():
+        for q in range(4):
+            for y in range(2):
+                row = jx[q // 3, y : y + 1] if q in (0, 3) else jm[q - 1, y : y + 1]
+                inv = jnp.broadcast_to(1.0 / row, (8, LANES))
+                rj[q, y] = inv
+                if q in (1, 2):
+                    rj2[q - 1, y] = inv * inv
+        for x in range(2):
+            sides = []
+            for s in range(2):
+                row = yr[0, 0, s, 8 * x + 6 : 8 * x + 7, 0:1]
+                row = jnp.broadcast_to(1.0 / jnp.where(row == 0.0, 1.0, row), (8, LANES))
+                rjh[s, x] = row
+                sides.append(row)
+            rjl[x] = jnp.where(left, sides[0], sides[1])
 
     def halos(t, f):
         inside = lane <= fz
@@ -315,25 +317,25 @@
 
             d = north(own[0]) - south(own[0])
             for c in range(3):
-                put(c, own[0][3 + c : 4 + c])
-            put(3, cross[2][4:5])
-            put(4, cross[2][3:4] + d[5:6])
-            put(5, d[4:5])
+                put(c, own[0][(2, 3, 5)[c] :][0:1])
+            put(3, cross[2][3:4])
+            put(4, cross[2][2:3] + d[5:6])
+            put(5, d[3:4])
             for x in range(2):
                 v = jnp.where(inside, own[x], 0.0)
                 d = (north(v) - south(v)) * rjh[s, x]
                 k = 6 + 6 * x
                 for c in range(3):
-                    put(k + c, own[x][c : c + 1])
+                    put(k + c, own[x][(0, 1, 4)[c] :][0:1])
                 put(k + 3, cross[x][1:2])
-                put(k + 4, cross[x][0:1] + d[2:3])
+                put(k + 4, cross[x][0:1] + d[4:5])
                 put(k + 5, d[1:2])
         tt[...] = jnp.transpose(gt[...])
 
     def item(v, k):
         return pltpu.roll(v, LANES - 1 - 2 * k, 1)
 
-    def coarse(t, f):
+    def coarse(t, f, other):
         for v in range(cz // 8):
             r = TOP + 8 * v
             th = tt[8 * v + 1 : 8 * v + 9, :]
@@ -377,23 +379,25 @@
                     cn[t + 1, i, r : r + 8, :] = new
                 else:
                     cout[i, 8 * v : 8 * v + 8, :] = new
-                if f == 1:
+                if other is not None:
+                    o = 3 * other + c
                     if t < STEPS - 1:
-                        pair = cn[t + 1, c, r : r + 8, :]
+                        pair = cn[t + 1, o, r : r + 8, :]
                     else:
-                        pair = cout[c, 8 * v : 8 * v + 8, :]
+                        pair = cout[o, 8 * v : 8 * v + 8, :]
                     prod = pair * new if prod is None else prod + pair * new
-            if f == 1:
+            if other is not None:
                 if t > 0:
                     prod = prod + cker[8 * v : 8 * v + 8, :]
                 cker[8 * v : 8 * v + 8, :] = prod
 
     def ghost(t, f):
+        at = (2, 3, 0)
         for c in range(3):
             i = 3 * f + c
-            gs[0, 3 + c : 4 + c] = xc[t, 0, i, TOP : TOP + 1, :]
-            gs[1, 3 + c : 4 + c] = cn[t, i, TOP : TOP + 1, :]
-            gs[2, 3 + c : 4 + c] = xc[t, 1, i, TOP : TOP + 1, :]
+            gs[0, at[c] : at[c] + 1] = xc[t, 0, i, TOP : TOP + 1, :]
+            gs[1, at[c] : at[c] + 1] = cn[t, i, TOP : TOP + 1, :]
+            gs[2, at[c] : at[c] + 1] = xc[t, 1, i, TOP : TOP + 1, :]
         flat = [gs[k] for k in range(3)]
         rim = []
         for tiles in (
@@ -401,7 +405,10 @@
             [yr[t, f, s, 0:8] for s in range(2)],
             [xk[t, f, 1, s] for s in range(2)],
         ):
-            rim.append(jnp.where(left, spread(tiles[0], 1, 8), spread(tiles[1], 1, 8)))
+            ends = [
+                jnp.where(sub == 0, spread(v, LANES - 1, 8), spread(v, 1, 8)) for v in tiles
+            ]
+            rim.append(jnp.where(left, ends[0], ends[1]))
 
         def mix(v):
             lo, mid, hi = v
@@ -422,15 +429,15 @@
                 for c in range(3):
                     i = 3 * f + c
                     if q in (0, 3):
-                        xf[t, q // 3, i, y, low_f : low_f + 1, :] = g[3 + c : 4 + c]
+                        xf[t, q // 3, i, y, low_f : low_f + 1, :] = g[at[c] : at[c] + 1]
                     else:
-                        fn[t, q - 1, i, y, low_f : low_f + 1, :] = g[3 + c : 4 + c]
+                        fn[t, q - 1, i, y, low_f : low_f + 1, :] = g[at[c] : at[c] + 1]
             if q in (1, 2):
                 g = jnp.where(y_edge, 0.75 * h + 0.25 * v, 0.0) * rjl[q - 1]
-                cor[q - 1, 0, 7:8] = g[5:6]
-                cor[q - 1, 1, 7:8] = g[4:5]
-
-    def fine(t, f):
+                cor[q - 1, 0, 7:8] = g[0:1]
+                cor[q - 1, 1, 7:8] = g[3:4]
+
+    def fine(t, f, other):
         for side in range(2):
             for c in (0, 2):
                 for y in range(2):
@@ -513,13 +520,14 @@
                             fn[t + 1, x, i, y, r : r + 8, :] = new
                         else:
                             fout[i, pick, :] = new
-                        if f == 1:
+                        if other is not None:
+                            o = 3 * other + c
                             if t < STEPS - 1:
-                                pair = fn[t + 1, x, c, y, r : r + 8, :]
+                                pair = fn[t + 1, x, o, y, r : r + 8, :]
                             else:
-                                pair = fout[c, pick, :]
+                                pair = fout[o, pick, :]
                             prod = pair * new if prod is None else prod + pair * new
-                    if f == 1:
+                    if other is not None:
                         if t > 0:
                             prod = prod + fker[pick, :]
                         fker[pick, :] = prod
@@ -529,41 +537,47 @@
             for x in range(2):
                 copy_top(t, x, 3 * f + c)
         ridge(t, f)
-        x_send(t, f, 0, 1)
+        x_send(t, f, 0)
+        x_send(t, f, 1, where=f == 0 or jnp.logical_not(middle))
         pack(t, f)
         y_send(t, f)
 
     for t in range(STEPS):
-        for f in range(2):
-            if f == 1:
-                pass_on(t, (2, 1)[t])
-            x_wait(t, f, 0)
-            if t == 0 and f == 0:
-                drain(ins.at[5], 8 * cz)
-            x_wait(t, f, 2)
-            halos(t, f)
-            coarse(t, f)
-            if t > 0 and f == 0:
+        for n in range(2):
+            for m in {(0, 0): (1,), (0, 1): (2, 3), (1, 0): (0,), (1, 1): ()}[t, n]:
+                pass_on(t, m)
+            if t > 0 and n == 0:
                 y_wait(t, 1)
                 x_send(t, 1, 2)
-            if t < STEPS - 1 and f == 1:
+                x_send(t, 1, 1, where=middle)
+            f = n if t < STEPS - 1 else (turn, 1 - turn)[n]
+            other = None if n == 0 else 1 - f
+            x_wait(t, f, 0)
+            if t == 0 and n == 0:
+                spacings()
+                drain(ins.at[2], 8 * cz)
+            if t > 0 and n == 0:
+                pass_on(1, 1)
+            halos(t, f)
+            coarse(t, f, other)
+            if t < STEPS - 1 and n == 1:
                 y_wait(t + 1, 0)
                 x_send(t + 1, 0, 2)
             ghost(t, f)
-            pass_on(t, ((1, 3), (0, 2))[t][f])
             x_wait(t, f, 1)
-            if t == 0 and f == 0:
-                drain(ins.at[6], 32 * fz)
-            fine(t, f)
+            if t == 0 and n == 0:
+                drain(ins.at[3], 32 * fz)
+            fine(t, f, other)
             if t < STEPS - 1:
                 finish_level(t + 1, f)
 
-    sent = 8 + 2 * STEPS * (3 * (cz + 1) + 6 * fz + 16)
+    sent = 8 + 2 * STEPS * (3 * (cz + 1) + 6 * fz + 8)
     each(has_x, lambda d: drain(xs.at[d], sent))
     each(has_y, lambda d: drain(ys.at[d], 32 * STEPS))
-    for t in range(STEPS):
-        for m in route[t]:
-            pl.when(passes[t][m])(pass_copy(t, m, 0).wait_send)
+    for k, n in enumerate(share):
+        taken = [m for r in route for m, least in r.items() if n >= least]
+        rows = sum(6 * fz if m % 2 else 3 * (cz + 1) for m in taken)
+        pl.when(middle & (rank == k))(functools.partial(drain, vs.at[0], rows))
 
 
 def put_body(*refs):
@@ -653,14 +667,13 @@
             pltpu.VMEM((4 * STEPS * (3 * cz + 6 * fz + 32), LANES), f32),
             pltpu.VMEM((STEPS, 2, 3, 2, fz, LANES), f32),
             pltpu.VMEM((STEPS, 2, 3, cz + 8, LANES), f32),
-            dma((7,)),
+            dma((4,)),
             dma((2,)),
-            dma((STEPS, 2, 3, 2)),
-            dma((2,)),
+            dma((STEPS, 2, 2, 2)),
             dma((2,)),
             dma((STEPS, 2, 2)),
-            dma((STEPS, 4)),
-            dma((STEPS, 4)),
+            dma((1,)),
+            dma((6,)),
         ],
         compiler_params=pltpu.CompilerParams(
             collective_id=0, has_side_effects=True, vmem_limit_bytes=32 << 20

time: 29.8 us -> 26.8 us (0.90)
  the two profiles are of different devices: /device:TPU:19 before, /device:TPU:9 now
where the time goes in v5:
time: 26.8 us; the launch traced here: 26.6 us
  Pallas kernels  26 us (97%)
  between operations  0.64 us (2%)
    pallas_call x1, Pallas kernels, on_device(): pl.pallas_call(functools.partial(body, nx, ny, fz, cz), out_shape=tuple((...  25 us
    pallas_call x1, Pallas kernels, on_device(): pl.pallas_call(put_body, out_shape=tuple((jax.ShapeDtypeStruct(s, f32) fo...  0.93 us

profile of v5, /device:TPU:9, one launch (start us, length us, event | category | flops | bytes accessed | tf_op | source)
XLA Modules:
  0.0 26.6 jit_solution(10899839323741300586)
XLA Ops:
  0.6 25.0 %wave.1 = (f32[6,160,128]{2,1,0:T(8,128)S(1)}, f32[6,80,128]{2,1,0:T(8,128)S(1)}, f32[160,128]{1,0:T(8,128)S(1)}, f32[80,128]{1,0:T(8,128)S(1)}) custom-call(f32[6,160,128]{2,1,0:T(8,128)} %bitcast.40, f32[6,160,128]{2,1,0:T(8,128)} %bitcast.41, f32[6,80,128]{2,1,0:T(8,128)} %bitcast.42, f32[6,80,128]{2,1,0:T(8,128)} %bitcast.43, f32[160,128]{1,0:T(8,128)} %bitcast.44, ...), custom_call_target="tpu_custom_call" | custom-call | tf_op jit(solution)/shard_map/wave/pallas_call | solution.py:635
  25.7 0.9 %put.1 = (f32[6,160,128]{2,1,0:T(8,128)}, f32[6,80,128]{2,1,0:T(8,128)}, f32[160,128]{1,0:T(8,128)}, f32[80,128]{1,0:T(8,128)}) custom-call(f32[6,160,128]{2,1,0:T(8,128)S(1)} %get-tuple-element.12.refs_0_, f32[6,80,128]{2,1,0:T(8,128)S(1)} %get-tuple-element.13.refs_1_, f32[160,128]{1,0:T(8,128)S(1)} %get-tuple-element.14.refs_2_, ...), custom_call_target="tpu_custom_call" | custom-call | tf_op jit(solution)/shard_map/put/pallas_call | solution.py:683

commit v6 on v5

--- a/solution.py
+++ b/solution.py
@@ -51,8 +51,6 @@
         "lf": (laf, lf),
     }
     slots = {"f0": 0, "c0": 0, "topo": 0, "f1": 1, "c1": 1, "co": 2, "sc": 2, "lc": 2}
-    for k, (a, b) in loads.items():
-        pltpu.make_async_copy(a, b, ins.at[slots.get(k, 3)]).start()
 
     def drain(sem, rows):
         part = span.at[pl.ds(0, rows)]
@@ -60,17 +58,28 @@
 
     planes = nx // 4 if nx % 4 == 0 else 0
     share = [min(3, (8 * (planes - 1 - z) + planes) // (2 * planes)) for z in range(planes - 1)]
-    route = [{1: 3, 2: 2, 3: 1}, {0: 2, 1: 1}]
-    reach = [{m: sum(n >= least for n in share) for m, least in r.items()} for r in route]
+    route = (
+        (0, 0, 2, 3, 3), (0, 1, 0, 3, 3), (0, 2, 0, 3, 2), (0, 3, 0, 3, 1),
+        (1, 0, 0, 1, 3), (1, 0, 1, 3, 2), (1, 1, 0, 3, 1),
+    )
+    reach = [sum(n >= least for n in share) for *_, least in route]
     at4, plane = lax.rem(gx, 4), gx // 4
     rank = jnp.where((at4 == 1) | (at4 == 3), plane, planes - 1 - plane)
     outer = ((at4 == 0), (at4 == 3))
     middle = (at4 == 1) | (at4 == 2)
-    detour = [{(m, d): outer[d] & (rank < r[m]) for m in r for d in range(2)} for r in reach]
-    passes = [{m: middle & (rank < r[m]) for m in r} for r in reach]
+    detour = [[outer[d] & (rank < r) for d in range(2)] for r in reach]
+    passes = [middle & (rank < r) for r in reach]
+
+    def parts(t, m):
+        cut = [(lo, hi, k) for k, (a, b, lo, hi, _) in enumerate(route) if (a, b) == (t, m)]
+        at, out = 0, []
+        for lo, hi, k in cut + [(3, 3, None)]:
+            out += [(at, lo, None)] if at < lo else []
+            out += [(lo, hi, k)] if lo < hi else []
+            at = hi
+        return out
     from_left = at4 == 2
-    even_x = lax.rem(gx, 2) == 0
-    turn = jnp.where((outer[0] & has_x[0]) | (outer[1] & has_x[1]), 1, 0) if share else 0
+    odd_x = lax.rem(gx, 2) == 1
 
     barrier = pltpu.get_barrier_semaphore()
     each(has_x, lambda d: pl.semaphore_signal(barrier, inc=1, device_id={"gx": gx + 2 * d - 1}))
@@ -81,52 +90,56 @@
         source = gx + jnp.where(from_left, -2, 2)
         pl.semaphore_signal(barrier, inc=1, device_id={"gx": source})
 
-    def x_copy(t, f, kind, d, land):
+    for k, (a, b) in loads.items():
+        pltpu.make_async_copy(a, b, ins.at[slots.get(k, 3)]).start()
+
+    def x_copy(t, f, kind, d, land, lo=0, hi=3):
+        some = pl.ds(3 * f + lo, hi - lo)
         if kind == 0:
             rows = pl.ds(TOP - 1, cz + 1)
-            src, dst = cn.at[t, half(f), rows], xc.at[t, land, half(f), rows]
+            src, dst = cn.at[t, some, rows], xc.at[t, land, some, rows]
         elif kind == 1:
             rows = pl.ds(TOP, fz)
-            src, dst = fn.at[t, d, half(f), :, rows], xf.at[t, land, half(f), :, rows]
+            src, dst = fn.at[t, d, some, :, rows], xf.at[t, land, some, :, rows]
         else:
             src, dst = yr.at[t, f, :, pl.ds(8 * d, 4)], xk.at[t, f, land, :, pl.ds(0, 4)]
         return pltpu.make_async_remote_copy(
             src, dst, xs.at[d], xr.at[t, f, kind % 2, land], device_id={"gx": gx + 2 * d - 1}
         )
 
-    def stop(t, m):
-        if m - 2 * (m // 2) == 1:
-            return via_f.at[t, m // 2]
-        return via_c.at[t, m // 2, :, pl.ds(0, cz + 1)]
-
-    def detour_copy(t, f, kind, d):
-        m = 2 * f + kind
-        if kind == 0:
-            src = cn.at[t, half(f), pl.ds(TOP - 1, cz + 1)]
-        else:
-            src = fn.at[t, d, half(f), :, pl.ds(TOP, fz)]
+    def ends_of(k, d, land):
+        t, m, lo, hi, _ = route[k]
+        some = pl.ds(3 * (m // 2) + lo, hi - lo)
+        if m % 2 == 0:
+            rows, stop = pl.ds(TOP - 1, cz + 1), via_c.at[t, m // 2, pl.ds(lo, hi - lo), pl.ds(0, cz + 1)]
+            return cn.at[t, some, rows], stop, xc.at[t, land, some, rows]
+        rows, stop = pl.ds(TOP, fz), via_f.at[t, m // 2, pl.ds(lo, hi - lo)]
+        return fn.at[t, d, some, :, rows], stop, xf.at[t, land, some, :, rows]
+
+    def detour_copy(k, d):
+        src, stop, _ = ends_of(k, d, 0)
         return pltpu.make_async_remote_copy(
-            src, stop(t, m), xs.at[d], vr.at[4 * t + m], device_id={"gx": gx + 2 - 4 * d}
+            src, stop, xs.at[d], vr.at[k], device_id={"gx": gx + 2 - 4 * d}
         )
 
-    def pass_copy(t, m, land):
-        f, kind = m // 2, m - 2 * (m // 2)
-        if kind == 0:
-            dst = xc.at[t, land, half(f), pl.ds(TOP - 1, cz + 1)]
-        else:
-            dst = xf.at[t, land, half(f), :, pl.ds(TOP, fz)]
+    def pass_copy(k, land):
+        t, m, *_ = route[k]
+        _, stop, dst = ends_of(k, 0, land)
         return pltpu.make_async_remote_copy(
-            stop(t, m), dst, vs.at[0], xr.at[t, f, kind, land],
+            stop, dst, vs.at[0], xr.at[t, m // 2, m % 2, land],
             device_id={"gx": gx + 3 - 6 * land},
         )
 
     def pass_on(t, m):
-        @pl.when(passes[t][m])
-        def _():
-            part = stop(t, m)
-            pltpu.make_async_copy(part, part, vr.at[4 * t + m]).wait()
-            for land in range(2):
-                pl.when((at4 == 1 + land))(pass_copy(t, m, land).start)
+        for k, (a, b, *_) in enumerate(route):
+            if (a, b) == (t, m):
+
+                @pl.when(passes[k])
+                def _():
+                    _, stop, _ = ends_of(k, 0, 0)
+                    pltpu.make_async_copy(stop, stop, vr.at[k]).wait()
+                    for land in range(2):
+                        pl.when(at4 == 1 + land)(pass_copy(k, land).start)
 
     def y_copy(t, f, d, land):
         return pltpu.make_async_remote_copy(
@@ -142,16 +155,20 @@
     def x_send(t, f, *kinds, where=True):
         def go(d):
             for kind in kinds:
-                m = 2 * f + kind
-                if kind == 2 or m not in route[t]:
+                if kind == 2:
                     x_copy(t, f, kind, d, 1 - d).start()
-                else:
-                    pl.when(detour[t][m, d])(detour_copy(t, f, kind, d).start)
-                    pl.when(jnp.logical_not(detour[t][m, d]))(x_copy(t, f, kind, d, 1 - d).start)
-
-        pl.when(has_x[1] & even_x & where)(functools.partial(go, 1))
+                    continue
+                for lo, hi, k in parts(t, 2 * f + kind):
+                    copy = x_copy(t, f, kind, d, 1 - d, lo, hi)
+                    if k is None:
+                        copy.start()
+                    else:
+                        pl.when(detour[k][d])(detour_copy(k, d).start)
+                        pl.when(jnp.logical_not(detour[k][d]))(copy.start)
+
+        pl.when(has_x[1] & odd_x & where)(functools.partial(go, 1))
         pl.when(has_x[0] & where)(functools.partial(go, 0))
-        pl.when(has_x[1] & jnp.logical_not(even_x) & where)(functools.partial(go, 1))
+        pl.when(has_x[1] & jnp.logical_not(odd_x) & where)(functools.partial(go, 1))
 
     def x_wait(t, f, kind):
         rows = 6 * fz if kind else 3 * (cz + 1) + 8 + (8 if t == 0 and f == 0 else 0)
@@ -544,20 +561,18 @@
 
     for t in range(STEPS):
         for n in range(2):
-            for m in {(0, 0): (1,), (0, 1): (2, 3), (1, 0): (0,), (1, 1): ()}[t, n]:
+            for m in {(0, 0): (0, 1), (0, 1): (2, 3), (1, 0): (0,), (1, 1): ()}[t, n]:
                 pass_on(t, m)
             if t > 0 and n == 0:
                 y_wait(t, 1)
                 x_send(t, 1, 2)
                 x_send(t, 1, 1, where=middle)
-            f = n if t < STEPS - 1 else (turn, 1 - turn)[n]
-            other = None if n == 0 else 1 - f
+                pass_on(1, 1)
+            f, other = n, None if n == 0 else 0
             x_wait(t, f, 0)
             if t == 0 and n == 0:
                 spacings()
                 drain(ins.at[2], 8 * cz)
-            if t > 0 and n == 0:
-                pass_on(1, 1)
             halos(t, f)
             coarse(t, f, other)
             if t < STEPS - 1 and n == 1:
@@ -575,8 +590,9 @@
     each(has_x, lambda d: drain(xs.at[d], sent))
     each(has_y, lambda d: drain(ys.at[d], 32 * STEPS))
     for k, n in enumerate(share):
-        taken = [m for r in route for m, least in r.items() if n >= least]
-        rows = sum(6 * fz if m % 2 else 3 * (cz + 1) for m in taken)
+        rows = sum(
+            (hi - lo) * (2 * fz if m % 2 else cz + 1) for _, m, lo, hi, least in route if n >= least
+        )
         pl.when(middle & (rank == k))(functools.partial(drain, vs.at[0], rows))
 
 
@@ -673,7 +689,7 @@
             dma((2,)),
             dma((STEPS, 2, 2)),
             dma((1,)),
-            dma((6,)),
+            dma((7,)),
         ],
         compiler_params=pltpu.CompilerParams(
             collective_id=0, has_side_effects=True, vmem_limit_bytes=32 << 20

time: 26.8 us -> 26.3 us (0.981)
  the two profiles are of different devices: /device:TPU:9 before, /device:TPU:19 now
where the time goes in v6:
time: 26.3 us; the launch traced here: 25.8 us
  Pallas kernels  25.1 us (95%)
  between operations  0.64 us (2%)
    pallas_call x1, Pallas kernels, on_device(): pl.pallas_call(functools.partial(body, nx, ny, fz, cz), out_shape=tuple((...  24.2 us
    pallas_call x1, Pallas kernels, on_device(): pl.pallas_call(put_body, out_shape=tuple((jax.ShapeDtypeStruct(s, f32) fo...  0.93 us

profile of v6, /device:TPU:19, one launch (start us, length us, event | category | flops | bytes accessed | tf_op | source)
XLA Modules:
  0.0 25.8 jit_solution(18290301178951677869)
XLA Ops:
  0.6 24.2 %wave.1 = (f32[6,160,128]{2,1,0:T(8,128)S(1)}, f32[6,80,128]{2,1,0:T(8,128)S(1)}, f32[160,128]{1,0:T(8,128)S(1)}, f32[80,128]{1,0:T(8,128)S(1)}) custom-call(f32[6,160,128]{2,1,0:T(8,128)} %bitcast.40, f32[6,160,128]{2,1,0:T(8,128)} %bitcast.41, f32[6,80,128]{2,1,0:T(8,128)} %bitcast.42, f32[6,80,128]{2,1,0:T(8,128)} %bitcast.43, f32[160,128]{1,0:T(8,128)} %bitcast.44, ...), custom_call_target="tpu_custom_call" | custom-call | tf_op jit(solution)/shard_map/wave/pallas_call | solution.py:651
  24.8 0.9 %put.1 = (f32[6,160,128]{2,1,0:T(8,128)}, f32[6,80,128]{2,1,0:T(8,128)}, f32[160,128]{1,0:T(8,128)}, f32[80,128]{1,0:T(8,128)}) custom-call(f32[6,160,128]{2,1,0:T(8,128)S(1)} %get-tuple-element.12.refs_0_, f32[6,80,128]{2,1,0:T(8,128)S(1)} %get-tuple-element.13.refs_1_, f32[160,128]{1,0:T(8,128)S(1)} %get-tuple-element.14.refs_2_, ...), custom_call_target="tpu_custom_call" | custom-call | tf_op jit(solution)/shard_map/put/pallas_call | solution.py:699

commit v7 on v6

--- a/solution.py
+++ b/solution.py
@@ -16,10 +16,10 @@
 def body(
     nx, ny, fz, cz,
     fold, fnow, cold, cnow, shf, laf, shc, lac, topo,
-    fout, cout, fker, cker,
-    fin, fo, co, sf, lf, sc, lc, tp,
-    fn, cn, xf, xc, jm, jx, pk, yr, xk,
-    rj, rj2, rjh, rjl, qs, gt, tt, gs, cor, span, via_f, via_c,
+    fout, cout, fker, cker, fn, xf, tt, rj, rj2, cor, sf, lf,
+    fin, fo, co, sc, lc, tp,
+    cn, xc, jm, jx, pk, yr, xk,
+    rjh, rjl, qs, gt, gs, span, via_f, via_c,
     ins, xs, xr, ys, yrs, vs, vr,
 ):
     f32 = jnp.float32
@@ -454,7 +454,7 @@
                 cor[q - 1, 0, 7:8] = g[0:1]
                 cor[q - 1, 1, 7:8] = g[3:4]
 
-    def fine(t, f, other):
+    def sides_top(t, f):
         for side in range(2):
             for c in (0, 2):
                 for y in range(2):
@@ -462,92 +462,29 @@
                         t, side, 3 * f + c, y, TOP : TOP + 1, :
                     ]
 
-        def plane(q, i, y, r):
+    def fine(t, f):
+        def plane(q, c, y, r):
+            i = 3 * f + c
             if q in (0, 3):
                 return xf[t, q // 3, i, y, r : r + 8, :]
             return fn[t, q - 1, i, y, r : r + 8, :]
 
-        for v in range(fz // 8):
-            r = TOP + 8 * v
-            th = tt[8 * v + 1 : 8 * v + 9, :]
-            for x in range(2):
-                q = x + 1
-                xx, yy, zz, up_down, twice = {}, {}, {}, {}, {}
-                va = [[None, None] for _ in range(3)]
-                tilt = {}
-                mid = {}
-                for y in range(2):
-                    inv = rj[q, y]
-                    cross, rise = [], []
-                    for c in range(3):
-                        i = 3 * f + c
-                        u = plane(q, i, y, r)
-                        e, w = plane(q + 1, i, y, r), plane(q - 1, i, y, r)
-                        dn, up = plane(q, i, y, r + 1), plane(q, i, y, r - 1)
-                        mid[c, y] = u
-                        u2 = 2.0 * u
-                        twice[c, y] = u2
-                        xx[c, y] = e + w - u2
-                        zz[c, y] = (dn + up - u2) * rj2[x, y]
-                        cross.append(e - w)
-                        rise.append((dn - up) * inv if c else None)
-                        if c != 1:
-                            ed, eu = plane(q + 1, i, y, r + 1), plane(q + 1, i, y, r - 1)
-                            wd, wu = plane(q - 1, i, y, r + 1), plane(q - 1, i, y, r - 1)
-                            tilt[c, y] = (ed - eu) * rj[q + 1, y] - (wd - wu) * rj[q - 1, y]
-                    va[0][y] = cross[1]
-                    va[1][y] = cross[0] + rise[2]
-                    va[2][y] = rise[1]
-
-                def ends(a, b, h):
-                    na, nb, sa, sb = north(a), north(b), south(a), south(b)
-                    return (
-                        (jnp.where(last, nb, na), jnp.where(first, h, sa)),
-                        (jnp.where(last, h, nb), jnp.where(first, sa, sb)),
-                    )
-
-                k = 6 + 6 * x
-                for c in range(3):
-                    for y, (n, s) in enumerate(ends(mid[c, 0], mid[c, 1], item(th, k + c))):
-                        yy[c, y] = n + s - twice[c, y]
-                ac = {}
-                for c in range(3):
-                    h = item(th, k + 3 + c)
-                    if c and v == fz // 8 - 1:
-                        h = h + cor[x, c - 1]
-                    for y, (n, s) in enumerate(ends(va[c][0], va[c][1], h)):
-                        ac[c, y] = n - s
-                for y in range(2):
-                    pick = pl.ds(32 * v + 2 * y + x, 8, stride=4)
-                    mu = STEP_SQUARED * sf[pick, :]
-                    both = STEP_SQUARED * lf[pick, :] + mu
-                    grad = (
-                        xx[0, y] + 0.25 * (ac[0, y] + tilt[2, y]),
-                        yy[1, y] + 0.25 * ac[1, y],
-                        zz[2, y] + 0.25 * (ac[2, y] + tilt[0, y]),
-                    )
-                    prod = None
-                    for c in range(3):
-                        i = 3 * f + c
-                        before = fo[i, pick, :] if t == 0 else fn[t - 1, x, i, y, r : r + 8, :]
-                        new = (twice[c, y] - before) + (
-                            mu * (xx[c, y] + yy[c, y] + zz[c, y]) + both * grad[c]
-                        )
-                        if t < STEPS - 1:
-                            fn[t + 1, x, i, y, r : r + 8, :] = new
-                        else:
-                            fout[i, pick, :] = new
-                        if other is not None:
-                            o = 3 * other + c
-                            if t < STEPS - 1:
-                                pair = fn[t + 1, x, o, y, r : r + 8, :]
-                            else:
-                                pair = fout[o, pick, :]
-                            prod = pair * new if prod is None else prod + pair * new
-                    if other is not None:
-                        if t > 0:
-                            prod = prod + fker[pick, :]
-                        fker[pick, :] = prod
+        def before(c, x, y, r, pick):
+            if t == 0:
+                return fo[3 * f + c, pick, :]
+            return fn[t - 1, x, 3 * f + c, y, r : r + 8, :]
+
+        def store(c, x, y, r, pick, new):
+            if t < STEPS - 1:
+                fn[t + 1, x, 3 * f + c, y, r : r + 8, :] = new
+            else:
+                fout[c, pick, :] = new
+
+        def product(x, y, r, pick, new):
+            if f == 1:
+                fker[pick, :] = sum(fn[t + 1, x, c, y, r : r + 8, :] * new[c] for c in range(3))
+
+        fine_update(fz, plane, before, store, product, tt, rj, rj2, cor, sf, lf)
 
     def finish_level(t, f):
         for c in range(3):
@@ -562,12 +499,15 @@
     for t in range(STEPS):
         for n in range(2):
             for m in {(0, 0): (0, 1), (0, 1): (2, 3), (1, 0): (0,), (1, 1): ()}[t, n]:
-                pass_on(t, m)
+                if (t, m) == (0, 3):
+                    pl.when(rank != len(share) - 1)(functools.partial(pass_on, t, m))
+                else:
+                    pass_on(t, m)
             if t > 0 and n == 0:
+                pass_on(1, 1)
                 y_wait(t, 1)
                 x_send(t, 1, 2)
                 x_send(t, 1, 1, where=middle)
-                pass_on(1, 1)
             f, other = n, None if n == 0 else 0
             x_wait(t, f, 0)
             if t == 0 and n == 0:
@@ -579,10 +519,14 @@
                 y_wait(t + 1, 0)
                 x_send(t + 1, 0, 2)
             ghost(t, f)
+            if t == 0 and n == 0:
+                pl.when(rank == len(share) - 1)(functools.partial(pass_on, 0, 3))
             x_wait(t, f, 1)
             if t == 0 and n == 0:
                 drain(ins.at[3], 32 * fz)
-            fine(t, f, other)
+            sides_top(t, f)
+            if (t, n) != (STEPS - 1, 1):
+                fine(t, f)
             if t < STEPS - 1:
                 finish_level(t + 1, f)
 
@@ -596,15 +540,114 @@
         pl.when(middle & (rank == k))(functools.partial(drain, vs.at[0], rows))
 
 
-def put_body(*refs):
-    ins, outs, sem = refs[:4], refs[4:8], refs[8]
-    copies = [
-        pltpu.make_async_copy(a, b, sem.at[i]) for i, (a, b) in enumerate(zip(ins, outs))
-    ]
-    for copy in copies:
-        copy.start()
-    for copy in copies:
-        copy.wait()
+def fine_update(fz, plane, before, store, product, tt, rj, rj2, cor, sf, lf, done=None):
+    lane = lax.broadcasted_iota(jnp.int32, (8, LANES), 1)
+    first, last = lane == 0, lane == LANES - 1
+
+    def ends(a, b, h):
+        na, nb = pltpu.roll(a, LANES - 1, 1), pltpu.roll(b, LANES - 1, 1)
+        sa, sb = pltpu.roll(a, 1, 1), pltpu.roll(b, 1, 1)
+        return (
+            (jnp.where(last, nb, na), jnp.where(first, h, sa)),
+            (jnp.where(last, h, nb), jnp.where(first, sa, sb)),
+        )
+
+    for v in range(fz // 8):
+        r = TOP + 8 * v
+        th = tt[8 * v + 1 : 8 * v + 9, :]
+        for x in range(2):
+            q, k = x + 1, 6 + 6 * x
+            mid, xx, yy, zz, twice, tilt, ac = {}, {}, {}, {}, {}, {}, {}
+            va = [[None, None] for _ in range(3)]
+            for y in range(2):
+                inv = rj[q, y]
+                cross, rise = [], []
+                for c in range(3):
+                    u = plane(q, c, y, r)
+                    e, w = plane(q + 1, c, y, r), plane(q - 1, c, y, r)
+                    dn, up = plane(q, c, y, r + 1), plane(q, c, y, r - 1)
+                    mid[c, y] = u
+                    u2 = 2.0 * u
+                    twice[c, y] = u2
+                    xx[c, y] = e + w - u2
+                    zz[c, y] = (dn + up - u2) * rj2[x, y]
+                    cross.append(e - w)
+                    rise.append((dn - up) * inv if c else None)
+                    if c != 1:
+                        ed, eu = plane(q + 1, c, y, r + 1), plane(q + 1, c, y, r - 1)
+                        wd, wu = plane(q - 1, c, y, r + 1), plane(q - 1, c, y, r - 1)
+                        tilt[c, y] = (ed - eu) * rj[q + 1, y] - (wd - wu) * rj[q - 1, y]
+                va[0][y] = cross[1]
+                va[1][y] = cross[0] + rise[2]
+                va[2][y] = rise[1]
+            for c in range(3):
+                h = pltpu.roll(th, LANES - 1 - 2 * (k + c), 1)
+                for y, (n, s) in enumerate(ends(mid[c, 0], mid[c, 1], h)):
+                    yy[c, y] = n + s - twice[c, y]
+            for c in range(3):
+                h = pltpu.roll(th, LANES - 1 - 2 * (k + 3 + c), 1)
+                if c and v == fz // 8 - 1:
+                    h = h + cor[x, c - 1]
+                for y, (n, s) in enumerate(ends(va[c][0], va[c][1], h)):
+                    ac[c, y] = n - s
+            for y in range(2):
+                pick = pl.ds(32 * v + 2 * y + x, 8, stride=4)
+                mu = STEP_SQUARED * sf[pick, :]
+                both = STEP_SQUARED * lf[pick, :] + mu
+                grad = (
+                    xx[0, y] + 0.25 * (ac[0, y] + tilt[2, y]),
+                    yy[1, y] + 0.25 * ac[1, y],
+                    zz[2, y] + 0.25 * (ac[2, y] + tilt[0, y]),
+                )
+                new = []
+                for c in range(3):
+                    new.append(
+                        (twice[c, y] - before(c, x, y, r, pick))
+                        + (mu * (xx[c, y] + yy[c, y] + zz[c, y]) + both * grad[c])
+                    )
+                    store(c, x, y, r, pick, new[c])
+                product(x, y, r, pick, new)
+        if done is not None:
+            done(v)
+
+
+def put_body(
+    fz, cz,
+    fa, ca, fk, ck, fn, xf, tt, rj, rj2, cor, sf, lf,
+    fout, cout, fker, cker,
+    fb, kb, span, sem,
+):
+    t = STEPS - 1
+
+    def write(a, b):
+        pltpu.make_async_copy(a, b, sem.at[0]).start()
+
+    write(fa, fout.at[pl.ds(0, 3)])
+    write(ca, cout)
+    write(ck, cker)
+
+    def plane(q, c, y, r):
+        if q in (0, 3):
+            return xf[t, q // 3, 3 + c, y, r : r + 8, :]
+        return fn[t, q - 1, 3 + c, y, r : r + 8, :]
+
+    def before(c, x, y, r, pick):
+        return fn[t - 1, x, 3 + c, y, r : r + 8, :]
+
+    def store(c, x, y, r, pick, new):
+        fb[c, pick, :] = new
+
+    def product(x, y, r, pick, new):
+        kb[pick, :] = fk[pick, :] + sum(fa[c, pick, :] * new[c] for c in range(3))
+
+    def done(v):
+        rows = pl.ds(32 * v, 32)
+        write(fb.at[:, rows], fout.at[pl.ds(3, 3), rows])
+
+    fine_update(fz, plane, before, store, product, tt, rj, rj2, cor, sf, lf, done)
+    write(kb, fker)
+    part = span.at[pl.ds(0, 28 * fz + 7 * cz)]
+    pltpu.make_async_copy(part, part, sem.at[0]).wait()
 
 
 def rows_view(a):
@@ -637,6 +680,9 @@
     vm = pl.BlockSpec(memory_space=pltpu.VMEM)
     hbm = pl.BlockSpec(memory_space=pl.ANY)
     shapes = ((6, nrows, LANES), (6, cz, cy), (nrows, LANES), (cz, cy))
+    planes = (STEPS, 2, 6, 2, fz + 16, LANES)
+    passed = ((3, nrows, LANES),) + shapes[1:] + (planes, planes, (LANES, LANES))
+    passed += ((4, 2, 8, LANES), (2, 2, 8, LANES), (2, 2, 8, LANES), shapes[2], shapes[2])
     args = (
         rows_view(fold),
         rows_view(fnow),
@@ -650,36 +696,28 @@
     )
     inner = pl.pallas_call(
         functools.partial(body, nx, ny, fz, cz),
-        out_shape=tuple(pltpu.VMEM(s, f32) for s in shapes),
+        out_shape=tuple(pltpu.VMEM(s, f32) for s in passed),
         in_specs=[hbm] * 9,
-        out_specs=(vm,) * 4,
+        out_specs=(vm,) * len(passed),
         scratch_shapes=[
             pltpu.VMEM((6, nrows, LANES), f32),
             pltpu.VMEM((6, nrows, LANES), f32),
             pltpu.VMEM((6, cz, cy), f32),
-            pltpu.VMEM((nrows, LANES), f32),
-            pltpu.VMEM((nrows, LANES), f32),
             pltpu.VMEM((cz, cy), f32),
             pltpu.VMEM((cz, cy), f32),
             pltpu.VMEM((fx, fy), jnp.int32),
-            pltpu.VMEM((STEPS, 2, 6, 2, fz + 16, LANES), f32),
             pltpu.VMEM((STEPS, 6, cz + 16, LANES), f32),
-            pltpu.VMEM((STEPS, 2, 6, 2, fz + 16, LANES), f32),
             pltpu.VMEM((STEPS, 2, 6, cz + 16, LANES), f32),
             pltpu.VMEM((2, 8, LANES), f32),
             pltpu.VMEM((2, 8, LANES), f32),
             pltpu.VMEM((STEPS, 2, 32, LANES), f32),
             pltpu.VMEM((STEPS, 2, 2, 16, LANES), f32),
             pltpu.VMEM((STEPS, 2, 2, 2, 8, LANES), f32),
-            pltpu.VMEM((4, 2, 8, LANES), f32),
-            pltpu.VMEM((2, 2, 8, LANES), f32),
             pltpu.VMEM((2, 2, 8, LANES), f32),
             pltpu.VMEM((2, 8, LANES), f32),
             pltpu.VMEM((LANES, LANES), f32),
             pltpu.VMEM((LANES, LANES), f32),
-            pltpu.VMEM((LANES, LANES), f32),
             pltpu.VMEM((3, 8, LANES), f32),
-            pltpu.VMEM((2, 2, 8, LANES), f32),
             pltpu.VMEM((4 * STEPS * (3 * cz + 6 * fz + 32), LANES), f32),
             pltpu.VMEM((STEPS, 2, 3, 2, fz, LANES), f32),
             pltpu.VMEM((STEPS, 2, 3, cz + 8, LANES), f32),
@@ -697,12 +735,17 @@
         name="wave",
     )(*[pltpu.with_memory_space_constraint(a, pltpu.HBM) for a in args])
     fout, cout, fker, cker = pl.pallas_call(
-        put_body,
+        functools.partial(put_body, fz, cz),
         out_shape=tuple(jax.ShapeDtypeStruct(s, f32) for s in shapes),
-        in_specs=[vm] * 4,
+        in_specs=[vm] * len(passed),
         out_specs=(hbm,) * 4,
-        scratch_shapes=[dma((4,))],
-        compiler_params=pltpu.CompilerParams(vmem_limit_bytes=1 << 20),
+        scratch_shapes=[
+            pltpu.VMEM((3, nrows, LANES), f32),
+            pltpu.VMEM((nrows, LANES), f32),
+            pltpu.VMEM((28 * fz + 7 * cz, LANES), f32),
+            dma((1,)),
+        ],
+        compiler_params=pltpu.CompilerParams(vmem_limit_bytes=4 << 20),
         name="put",
     )(*[pltpu.with_memory_space_constraint(a, pltpu.VMEM) for a in inner])
     return (

time: 26.3 us -> 26.1 us (level)
  the two profiles are of different devices: /device:TPU:19 before, /device:TPU:25 now
where the time goes in v7:
time: 26.1 us; the launch traced here: 25.9 us
  Pallas kernels  25.3 us (97%)
  between operations  0.64 us (2%)
    pallas_call x1, Pallas kernels, on_device(): pl.pallas_call(functools.partial(body, nx, ny, fz, cz), out_shape=tuple((...  24.2 us
    pallas_call x1, Pallas kernels, on_device(): pl.pallas_call(functools.partial(put_body, fz, cz), out_shape=tuple((jax....  1.08 us

profile of v7, /device:TPU:25, one launch (start us, length us, event | category | flops | bytes accessed | tf_op | source)
XLA Modules:
  0.0 25.9 jit_solution(13828018086918804142)
XLA Ops:
  0.6 24.2 %wave.1 = (f32[3,160,128]{2,1,0:T(8,128)S(1)}, f32[6,80,128]{2,1,0:T(8,128)S(1)}, f32[160,128]{1,0:T(8,128)S(1)}, f32[80,128]{1,0:T(8,128)S(1)}, f32[2,2,6,2,56,...) custom-call(f32[6,160,128]{2,1,0:T(8,128)} %bitcast.40, ...), custom_call_target="tpu_custom_call" | custom-call | tf_op jit(solution)/shard_map/wave/pallas_call | solution.py:697
  24.8 1.1 %put.1 = (f32[6,160,128]{2,1,0:T(8,128)}, f32[6,80,128]{2,1,0:T(8,128)}, f32[160,128]{1,0:T(8,128)}, f32[80,128]{1,0:T(8,128)}) custom-call(f32[3,160,128]{2,1,0:T(8,128)S(1)} %get-tuple-element.20.fa, f32[6,80,128]{2,1,0:T(8,128)S(1)} %get-tuple-element.21.ca, f32[160,128]{1,0:T(8,128)S(1)} %get-tuple-element.22.fk, f32[80,128]{1,0:T(8,128)S(1)} %get-tuple-element.23.ck, ...), custom_call_target="tpu_custom_call" | custom-call | tf_op jit(solution)/shard_map/put/pallas_call | solution.py:737

commit v8 on v7

--- a/solution.py
+++ b/solution.py
@@ -141,6 +141,24 @@
                     for land in range(2):
                         pl.when(at4 == 1 + land)(pass_copy(k, land).start)
 
+    def corner_copy(t, f, d, e):
+        return pltpu.make_async_remote_copy(
+            pk.at[t, f, pl.ds(16 * e + 8 * d, 4)], xk.at[t, f, 1 - d, 1 - e, pl.ds(0, 4)],
+            xs.at[d], xr.at[t, f, 0, 1 - d],
+            device_id={"gx": gx + 2 * d - 1, "gy": gy + 2 * e - 1},
+        )
+
+    def corner_send(t, f):
+        for d in range(2):
+            for e in range(2):
+                pl.when(has_x[d] & has_y[e])(corner_copy(t, f, d, e).start)
+
+    def drain_y(sem, rows, more):
+        both, some = has_y[0] & has_y[1], has_y[0] | has_y[1]
+        pl.when(both)(functools.partial(drain, sem, rows + 2 * more))
+        pl.when(some & jnp.logical_not(both))(functools.partial(drain, sem, rows + more))
+        pl.when(jnp.logical_not(some))(functools.partial(drain, sem, rows))
+
     def y_copy(t, f, d, land):
         return pltpu.make_async_remote_copy(
             pk.at[t, f, pl.ds(16 * d, 16)], yr.at[t, f, land], ys.at[d], yrs.at[t, f, land],
@@ -152,7 +170,7 @@
             jm.at[d], jx.at[land], xs.at[d], xr.at[0, 0, 0, land], device_id={"gx": gx + 2 * d - 1}
         )
 
-    def x_send(t, f, *kinds, where=True):
+    def x_send(t, f, *kinds):
         def go(d):
             for kind in kinds:
                 if kind == 2:
@@ -166,13 +184,16 @@
                         pl.when(detour[k][d])(detour_copy(k, d).start)
                         pl.when(jnp.logical_not(detour[k][d]))(copy.start)
 
-        pl.when(has_x[1] & odd_x & where)(functools.partial(go, 1))
-        pl.when(has_x[0] & where)(functools.partial(go, 0))
-        pl.when(has_x[1] & jnp.logical_not(odd_x) & where)(functools.partial(go, 1))
+        pl.when(has_x[1] & odd_x)(functools.partial(go, 1))
+        pl.when(has_x[0])(functools.partial(go, 0))
+        pl.when(has_x[1] & jnp.logical_not(odd_x))(functools.partial(go, 1))
 
     def x_wait(t, f, kind):
-        rows = 6 * fz if kind else 3 * (cz + 1) + 8 + (8 if t == 0 and f == 0 else 0)
-        each(has_x, lambda d: drain(xr.at[t, f, kind, d], rows))
+        rows = 6 * fz if kind else 3 * (cz + 1) + (0 if t else 8) + (8 if t == 0 and f == 0 else 0)
+        if t > 0 and kind == 0:
+            each(has_x, lambda d: drain_y(xr.at[t, f, kind, d], rows, 4))
+        else:
+            each(has_x, lambda d: drain(xr.at[t, f, kind, d], rows))
 
     def y_send(t, f):
         each(has_y, lambda d: y_copy(t, f, d, 1 - d).start())
@@ -228,6 +249,9 @@
             for t in range(STEPS):
                 for f in range(2):
                     yr[t, f, d] = jnp.zeros(yr.shape[3:], f32)
+                    if t > 0:
+                        for side in range(2):
+                            xk[t, f, side, d] = jnp.zeros(xk.shape[4:], f32)
 
     def ridge(t, f):
         for c in range(3):
@@ -492,9 +516,10 @@
                 copy_top(t, x, 3 * f + c)
         ridge(t, f)
         x_send(t, f, 0)
-        x_send(t, f, 1, where=f == 0 or jnp.logical_not(middle))
         pack(t, f)
         y_send(t, f)
+        corner_send(t, f)
+        x_send(t, f, 1)
 
     for t in range(STEPS):
         for n in range(2):
@@ -505,19 +530,15 @@
                     pass_on(t, m)
             if t > 0 and n == 0:
                 pass_on(1, 1)
-                y_wait(t, 1)
-                x_send(t, 1, 2)
-                x_send(t, 1, 1, where=middle)
             f, other = n, None if n == 0 else 0
             x_wait(t, f, 0)
             if t == 0 and n == 0:
                 spacings()
                 drain(ins.at[2], 8 * cz)
+            if t > 0:
+                y_wait(t, f)
             halos(t, f)
             coarse(t, f, other)
-            if t < STEPS - 1 and n == 1:
-                y_wait(t + 1, 0)
-                x_send(t + 1, 0, 2)
             ghost(t, f)
             if t == 0 and n == 0:
                 pl.when(rank == len(share) - 1)(functools.partial(pass_on, 0, 3))
@@ -530,8 +551,8 @@
             if t < STEPS - 1:
                 finish_level(t + 1, f)
 
-    sent = 8 + 2 * STEPS * (3 * (cz + 1) + 6 * fz + 8)
-    each(has_x, lambda d: drain(xs.at[d], sent))
+    sent = 8 + 16 + 2 * STEPS * (3 * (cz + 1) + 6 * fz)
+    each(has_x, lambda d: drain_y(xs.at[d], sent, 8 * (STEPS - 1)))
     each(has_y, lambda d: drain(ys.at[d], 32 * STEPS))
     for k, n in enumerate(share):
         rows = sum(

time: 26.1 us -> 25.7 us (0.985)
  the two profiles are of different devices: /device:TPU:25 before, /device:TPU:19 now
where the time goes in v8:
time: 25.7 us; the launch traced here: 25.5 us
  Pallas kernels  24.9 us (97%)
  between operations  0.64 us (2%)
    pallas_call x1, Pallas kernels, on_device(): pl.pallas_call(functools.partial(body, nx, ny, fz, cz), out_shape=tuple((...  23.8 us
    pallas_call x1, Pallas kernels, on_device(): pl.pallas_call(functools.partial(put_body, fz, cz), out_shape=tuple((jax....  1.08 us

profile of v8, /device:TPU:19, one launch (start us, length us, event | category | flops | bytes accessed | tf_op | source)
XLA Modules:
  0.0 25.5 jit_solution(12826655593744653500)
XLA Ops:
  0.6 23.8 %wave.1 = (f32[3,160,128]{2,1,0:T(8,128)S(1)}, f32[6,80,128]{2,1,0:T(8,128)S(1)}, f32[160,128]{1,0:T(8,128)S(1)}, f32[80,128]{1,0:T(8,128)S(1)}, f32[2,2,6,2,56,...) custom-call(f32[6,160,128]{2,1,0:T(8,128)} %bitcast.40, ...), custom_call_target="tpu_custom_call" | custom-call | tf_op jit(solution)/shard_map/wave/pallas_call | solution.py:718
  24.4 1.1 %put.1 = (f32[6,160,128]{2,1,0:T(8,128)}, f32[6,80,128]{2,1,0:T(8,128)}, f32[160,128]{1,0:T(8,128)}, f32[80,128]{1,0:T(8,128)}) custom-call(f32[3,160,128]{2,1,0:T(8,128)S(1)} %get-tuple-element.20.fa, f32[6,80,128]{2,1,0:T(8,128)S(1)} %get-tuple-element.21.ca, f32[160,128]{1,0:T(8,128)S(1)} %get-tuple-element.22.fk, f32[80,128]{1,0:T(8,128)S(1)} %get-tuple-element.23.ck, ...), custom_call_target="tpu_custom_call" | custom-call | tf_op jit(solution)/shard_map/put/pallas_call | solution.py:758
